TPU v7x, 128 devices: a whole 4x4x4 slice. The times are simulated.
128 devices in a mesh: seq: 32 (over x, z, core), head: 4 (over y).
Axes of the slice: x: 4, y: 4, z: 4, core: 2. Of those that a mesh axis runs over, the one named last changes fastest.
Arguments:
- queries: bfloat16 [32768, 2048], P('seq', 'head'), may hold values from -64 to 64
- keys: bfloat16 [32768, 2048], P('seq', 'head'), may hold values from -16 to 16
- values: bfloat16 [32768, 2048], P('seq', 'head'), may hold values from -6 to 6
- span_bounds: int32 [64, 2], replicated, may hold values from 0 to 32768, as said below
- mem_decay: float32 [32, 16], P(None, 'head'), may hold values from 0.01 to 1
- mem_gate: float32 [16], P('head'), may hold values from -2 to 2
- out_weight: bfloat16 [2048, 4096], P('head'), may hold values from -0.125 to 0.125
Outputs:
- mixed: bfloat16 [32768, 4096], P('seq', 'head')
Inputs may be any that keep to these rules, and one draw needn't show every extreme that they name: `span_bounds`: slot k lies in segment k // 2, inside the k % 2-th of 2 equal parts of it; start <= end, an empty slot has start == end; some slot covers a whole part.
All inputs are finite; a program needn't handle non-finite values.
Results may differ from a plain program's by a relative error of at most 0.0052.
The roundings to bfloat16 on the way count: a program that leaves them out, or rounds other values in their place, can miss the bound.
Values may be sent and summed in bfloat16 or wider, within the bound.
A program may use at most 128 MiB of HBM per device.

v0:
```python
import math

import jax
import jax.numpy as jnp
from jax import lax
from jax.sharding import PartitionSpec as P

BAND = 512
SPAN_DEV = 2


HIGHEST_PRECISION = lax.Precision.HIGHEST


def from_behind(block, axis, distance):
    devices = range(lax.axis_size(axis))
    route = [(i - distance, i) for i in devices if i - distance in devices]
    return lax.ppermute(block, axis, route)


def side_by_side(arrays, axis, dim, along):
    columns = [a.reshape(*a.shape[:along], -1) for a in arrays]
    both = jnp.concatenate(columns, axis=along)
    whole, at, outs = (lax.all_gather(both, axis, axis=dim, tiled=True), 0, [])
    for a, column in zip(arrays, columns):
        section = whole[..., at : at + column.shape[along]]
        outs.append(section.reshape(*section.shape[:along], *a.shape[along:]))
        at += column.shape[along]
    return tuple(outs)


def in_order(pieces, dim):
    pieces = jnp.moveaxis(pieces, 0, dim)
    dims = pieces.shape
    return pieces.reshape(*dims[:dim], dims[dim] * dims[dim + 1], *dims[dim + 2 :])


def sent_to_all(shard, axis):
    copies = jnp.broadcast_to(shard, (lax.axis_size(axis), *shard.shape))
    return lax.all_to_all(copies, axis, split_axis=0, concat_axis=0, tiled=True)


def gathered_copies(shard, axis, dim):
    return in_order(sent_to_all(shard, axis), dim)


def feature_map(values_in):
    return jnp.where(values_in > 0, values_in + 1.0, jnp.exp(jnp.minimum(values_in, 0.0)))


def local_attention(
    queries_3d, band_keys, band_values, query_labels, key_labels, shard_index, band_width
):
    seg_rows, head_count, head_width = queries_3d.shape
    block_rows = min(seg_rows, 512)
    key_count = band_keys.shape[0]
    key_pos = jnp.arange(key_count) - band_width
    key_valid = (key_pos >= 0) | (shard_index > 0)
    score_scale = 1.0 / math.sqrt(head_width)

    def attend_block(block_index):
        row_start = block_index * block_rows
        query_block = lax.dynamic_slice_in_dim(queries_3d, row_start, block_rows, 0)
        label_block = lax.dynamic_slice_in_dim(query_labels, row_start, block_rows, 0)
        query_pos = row_start + jnp.arange(block_rows)
        scores = (
            jnp.einsum("qhd,khd->hqk", query_block, band_keys, preferred_element_type=jnp.float32)
            * score_scale
        )
        nearby = (
            (key_pos[None, :] <= query_pos[:, None])
            & (key_pos[None, :] > query_pos[:, None] - band_width)
            & key_valid[None, :]
        )
        same_span = (label_block[:, None] > 0) & (label_block[:, None] == key_labels[None, :])
        visible = nearby | same_span
        scores = jnp.where(visible[None], scores, -1e30)
        top_score = jnp.max(scores, axis=-1, keepdims=True)
        weights = jnp.exp(scores - top_score)
        totals = jnp.sum(weights, axis=-1)
        mixed_out = jnp.einsum(
            "hqk,khd->qhd",
            weights.astype(jnp.bfloat16),
            band_values,
            preferred_element_type=jnp.float32,
        )
        return mixed_out / jnp.transpose(totals)[:, :, None]

    blocks = lax.map(attend_block, jnp.arange(seg_rows // block_rows))
    return blocks.reshape(seg_rows, head_count, head_width)


def body(queries, keys, values, span_bounds, mem_decay, mem_gate, out_weight):
    seg_rows = queries.shape[0]
    head_count = mem_gate.shape[0]
    head_width = queries.shape[1] // head_count
    band_width = BAND
    shard_index = lax.axis_index("seq")
    prev_keys, prev_values = from_behind(
        (keys[seg_rows - band_width :], values[seg_rows - band_width :]), "seq", 1
    )
    key_feats = feature_map(keys.astype(jnp.float32)).reshape(seg_rows, head_count, head_width)
    value_rows = values.astype(jnp.float32).reshape(seg_rows, head_count, head_width)
    state = jnp.einsum("thd,the->hde", key_feats, value_rows, precision=HIGHEST_PRECISION)
    feat_sum = jnp.sum(key_feats, axis=0)
    cumulative = jnp.cumsum(jnp.log(mem_decay), axis=0)
    before = lax.dynamic_index_in_dim(
        cumulative, jnp.maximum(shard_index - 1, 0), 0, keepdims=False
    )
    part_state, part_sum = side_by_side((state[None], feat_sum[None]), "seq", 0, 3)
    piece_count = part_state.shape[0]
    piece_index = jnp.arange(piece_count)
    factor = jnp.where(
        (piece_index < shard_index)[:, None],
        jnp.exp(jnp.minimum(before[None, :] - cumulative, 0.0)),
        0.0,
    )
    memory = jnp.einsum("nh,nhde->hde", factor, part_state, precision=HIGHEST_PRECISION)
    feat_total = jnp.einsum("nh,nhd->hd", factor, part_sum, precision=HIGHEST_PRECISION)
    query_feats = feature_map(queries.astype(jnp.float32)).reshape(seg_rows, head_count, head_width)
    numer = jnp.einsum("thd,hde->the", query_feats, memory, precision=HIGHEST_PRECISION)
    denom = jnp.einsum("thd,hd->th", query_feats, feat_total, precision=HIGHEST_PRECISION) + 1.0
    readout = numer / denom[:, :, None]
    own_spans = lax.dynamic_slice_in_dim(span_bounds, shard_index * SPAN_DEV, SPAN_DEV, 0)
    positions = shard_index * seg_rows + jnp.arange(seg_rows)
    inside = (positions[:, None] >= own_spans[None, :, 0]) & (
        positions[:, None] < own_spans[None, :, 1]
    )
    slot_ids = (jnp.arange(SPAN_DEV) + 1)[None, :]
    query_labels = jnp.sum(inside.astype(jnp.int32) * slot_ids, axis=1)
    key_labels = jnp.concatenate([jnp.zeros((band_width,), jnp.int32), query_labels])
    band_keys = jnp.concatenate([prev_keys, keys], axis=0).reshape(
        band_width + seg_rows, head_count, head_width
    )
    band_values = jnp.concatenate([prev_values, values], axis=0).reshape(
        band_width + seg_rows, head_count, head_width
    )
    queries_3d = queries.reshape(seg_rows, head_count, head_width)
    local = local_attention(
        queries_3d, band_keys, band_values, query_labels, key_labels, shard_index, band_width
    )
    gate = jax.nn.sigmoid(mem_gate)[None, :, None]
    attended = (
        (gate * readout + (1.0 - gate) * local)
        .astype(jnp.bfloat16)
        .reshape(seg_rows, head_count * head_width)
    )
    gathered = gathered_copies(attended, "head", 1)
    columns = lax.all_to_all(out_weight, "head", split_axis=1, concat_axis=0, tiled=True)
    mixed = jnp.dot(gathered, columns, preferred_element_type=jnp.float32)
    return mixed.astype(jnp.bfloat16)


def solution(mesh):
    return jax.shard_map(
        body,
        mesh=mesh,
        in_specs=(
            P("seq", "head"),
            P("seq", "head"),
            P("seq", "head"),
            P(),
            P(None, "head"),
            P("head"),
            P("head", None),
        ),
        out_specs=P("seq", "head"),
        check_vma=False,
    )
```

profile of v0, /device:TPU:4, one launch (start us, length us, event | category | flops | bytes accessed | tf_op | source)
XLA Modules:
  0.0 206.4 jit_solution(12153118912402493625)
XLA Ops:
  11.7 1.9 collective-permute-start.1
  15.0 3.9 %collective-permute-start = (bf16[512,512]{0,1:T(8,128)(2,1)}, bf16[512,512]{0,1:T(8,128)(2,1)}, u32[]{:S(2)}, u32[]{:S(2)}) collective-permute-start(bf16[512,512]{0,1:T(8,128)(2,1)} %slice.26), channel_id=1, source_target_pairs={{0,4},{4,8},{8,12},{12,16},{16,20},{20,24},{24,28},{28,32},{32,36}... | collective-permute-start | bytes 1572872 | tf_op jit(solution)/shard_map/ppermute | solution.py:18
  19.0 6.5 %copy.62 = bf16[512,4096]{0,1:T(8,128)(2,1)} copy(bf16[512,4096]{1,0:T(8,128)(2,1)} %param.15) | data formatting | bytes 8388608 | tf_op args[6]
  25.5 6.3 %copy.63 = bf16[512,4,1024]{2,0,1:T(8,128)(2,1)} copy(bf16[512,4,1024]{0,2,1:T(8,128)(2,1)} %bitcast.96) | data formatting | bytes 8388608 | tf_op jit(solution)/shard_map/all_to_all | solution.py:149
  31.8 5.2 %all-to-all-start.1 = ((bf16[512,4,1024]{2,0,1:T(8,128)(2,1)}), bf16[512,4,1024]{2,0,1:T(8,128)(2,1)}, u32[]{:S(2)}, u32[]{:S(2)}) async-start(bf16[512,4,1024]{2,0,1:T(8,128)(2,1)} %copy.63), calls=%async_computation.1 | async-start | bytes 8388608 | tf_op jit(solution)/shard_map/all_to_all | solution.py:149
  37.4 1.7 fusion.27
  39.2 2.3 %copy.52 = bf16[1024,512]{0,1:T(8,128)(2,1)} copy(bf16[1024,512]{1,0:T(8,128)(2,1)} %param.9) | data formatting | bytes 2097152 | tf_op args[0]
  41.6 1.8 copy.84
  48.3 75.2 %while.14 = (s32[]{:T(128)}, f32[2,512,4,128]{1,0,3,2:T(2,128)}, s32[2]{0:T(128)S(1)}, s32[1024]{0:T(1024)S(1)}, s32[1536]{0:T(1024)S(1)}, /*index=5*/bf16[1024,...) while((s32[]{:T(128)}, f32[2,512,4,128]{1,0,3,2:T(2,128)}, ...), condition=%wide.region_6.7_spmd.clone.clone, body=%wide.region_3.6_spmd.clone.clone.sunk | while | flops 1650986496 | bytes 56176868 | solution.py:89
  51.2 4.1 %fusion.66 = (f32[4,512]{1,0:T(4,128)S(1)}, f32[4,512,1536]{2,1,0:T(8,128)S(1)}) fusion(pred[512,1536]{1,0:T(8,128)(4,1)S(1)} %and_or_fusion.2, bf16[1536,4,128]{2,0,1:T(8,128)(2,1)S(1)} %get-tuple-element.338, bf16[1024,4,128]{0,2,1:T(8,128)(2,1)} %get-tuple-element.337, s32[]{:T(128)S(6)} %select_n.70), kind=kOutput, calls=%fused_computation.4.clone.1 | convolution fusion | flops 814741504 | bytes 15474692 | tf_op jit(solution)/shard_map/while/body/eval_jaxpr/qhd,khd->hqk/dot_general | solution.py:67
  55.4 3.6 %fusion.67 = f32[4,512]{1,0:T(4,128)S(1)} fusion(f32[4,512,1536]{2,1,0:T(8,128)S(1)} %get-tuple-element.304, f32[4,512]{1,0:T(4,128)S(1)} %get-tuple-element.305, pred[512,1536]{1,0:T(8,128)(4,1)S(1)} %and_or_fusion.2), kind=kLoop, calls=%fused_computation.5.clone.1 | loop fusion | flops 12580864 | bytes 13385728 | tf_op jit(solution)/shard_map/while/body/eval_jaxpr/reduce_sum | solution.py:80
  59.0 4.9 %divide_bitcast_fusion.2 = f32[1,512,4,128]{3,1,2,0:T(8,128)} fusion(bf16[1536,4,128]{2,0,1:T(8,128)(2,1)S(1)} %copy-done.7, f32[4,512,1536]{2,1,0:T(8,128)S(1)} %get-tuple-element.304, f32[4,512]{1,0:T(4,128)S(1)} %get-tuple-element.305, pred[512,1536]{1,0:T(8,128)(4,1)S(1)} %and_or_fusion.2, f32[512,4]{0,1:T(4,128)S(1)} %bitcast.103), kind=kOutput, calls=%fused_computation.11.clone.1 | convolution fusion | flops 818151424 | bytes 16007168 | tf_op jit(solution)/shard_map/while/body/eval_jaxpr/hqk,khd->qhd/dot_general | solution.py:81
  63.9 2.4 %copy.98 = f32[1,512,4,128]{1,0,3,2:T(1,128)S(1)} copy(f32[1,512,4,128]{3,1,2,0:T(8,128)} %divide_bitcast_fusion.2) | data formatting | bytes 2097152 | tf_op jit(solution)/shard_map/while/body/jit(dynamic_update_index_in_dim)/dynamic_update_slice | solution.py:89
  66.3 19.6 %dynamic_update_slice.10 = f32[2,512,4,128]{1,0,3,2:T(2,128)} dynamic-update-slice(f32[2,512,4,128]{1,0,3,2:T(2,128)} %get-tuple-element.320, f32[1,512,4,128]{1,0,3,2:T(1,128)S(1)} %copy.98, s32[]{:T(128)} %get-tuple-element.319, s32[]{:T(128)} %constant.90.clone.1..sunk, s32[]{:T(128)} %constant.90.clone.1..sunk, s32[]{:T(128)} %constant.90.clone.1..sunk) | dynamic-update-slice | bytes 2097156 | tf_op jit(solution)/shard_map/while/body/jit(dynamic_update_index_in_dim)/dynamic_update_slice | solution.py:89
  88.8 4.1 %fusion.66 = (f32[4,512]{1,0:T(4,128)S(1)}, f32[4,512,1536]{2,1,0:T(8,128)S(1)}) fusion(pred[512,1536]{1,0:T(8,128)(4,1)S(1)} %and_or_fusion.2, bf16[1536,4,128]{2,0,1:T(8,128)(2,1)S(1)} %get-tuple-element.338, bf16[1024,4,128]{0,2,1:T(8,128)(2,1)} %get-tuple-element.337, s32[]{:T(128)S(6)} %select_n.70), kind=kOutput, calls=%fused_computation.4.clone.1 | convolution fusion | flops 814741504 | bytes 15474692 | tf_op jit(solution)/shard_map/while/body/eval_jaxpr/qhd,khd->hqk/dot_general | solution.py:67
  93.0 3.6 %fusion.67 = f32[4,512]{1,0:T(4,128)S(1)} fusion(f32[4,512,1536]{2,1,0:T(8,128)S(1)} %get-tuple-element.304, f32[4,512]{1,0:T(4,128)S(1)} %get-tuple-element.305, pred[512,1536]{1,0:T(8,128)(4,1)S(1)} %and_or_fusion.2), kind=kLoop, calls=%fused_computation.5.clone.1 | loop fusion | flops 12580864 | bytes 13385728 | tf_op jit(solution)/shard_map/while/body/eval_jaxpr/reduce_sum | solution.py:80
  96.6 4.9 %divide_bitcast_fusion.2 = f32[1,512,4,128]{3,1,2,0:T(8,128)} fusion(bf16[1536,4,128]{2,0,1:T(8,128)(2,1)S(1)} %copy-done.7, f32[4,512,1536]{2,1,0:T(8,128)S(1)} %get-tuple-element.304, f32[4,512]{1,0:T(4,128)S(1)} %get-tuple-element.305, pred[512,1536]{1,0:T(8,128)(4,1)S(1)} %and_or_fusion.2, f32[512,4]{0,1:T(4,128)S(1)} %bitcast.103), kind=kOutput, calls=%fused_computation.11.clone.1 | convolution fusion | flops 818151424 | bytes 16007168 | tf_op jit(solution)/shard_map/while/body/eval_jaxpr/hqk,khd->qhd/dot_general | solution.py:81
  101.5 2.4 %copy.98 = f32[1,512,4,128]{1,0,3,2:T(1,128)S(1)} copy(f32[1,512,4,128]{3,1,2,0:T(8,128)} %divide_bitcast_fusion.2) | data formatting | bytes 2097152 | tf_op jit(solution)/shard_map/while/body/jit(dynamic_update_index_in_dim)/dynamic_update_slice | solution.py:89
  103.9 19.6 %dynamic_update_slice.10 = f32[2,512,4,128]{1,0,3,2:T(2,128)} dynamic-update-slice(f32[2,512,4,128]{1,0,3,2:T(2,128)} %get-tuple-element.320, f32[1,512,4,128]{1,0,3,2:T(1,128)S(1)} %copy.98, s32[]{:T(128)} %get-tuple-element.319, s32[]{:T(128)} %constant.90.clone.1..sunk, s32[]{:T(128)} %constant.90.clone.1..sunk, s32[]{:T(128)} %constant.90.clone.1..sunk) | dynamic-update-slice | bytes 2097156 | tf_op jit(solution)/shard_map/while/body/jit(dynamic_update_index_in_dim)/dynamic_update_slice | solution.py:89
  123.5 4.2 %reshape.184 = f32[1024,4,128]{0,2,1:T(8,128)} reshape(f32[2,512,4,128]{1,0,3,2:T(2,128)} %get-tuple-element.133) | data formatting | bytes 4194304 | tf_op jit(solution)/shard_map/reshape | solution.py:90
  129.8 5.6 %fusion.21 = f32[4,128,128]{1,0,2:T(4,128)S(1)} fusion(f32[32,4,128,129]{2,1,3,0:T(4,128)} %all-gather.2.cloned.1.call-done, f32[4,32]{0,1:T(8,128)S(1)} %get-tuple-element.235), kind=kLoop, calls=%fused_computation.24 | loop fusion | flops 4128768 | bytes 8651264
  135.5 2.1 %fusion.34 = bf16[1024,4,128]{0,2,1:T(8,128)(2,1)S(1)} fusion(f32[1024,4,128]{0,2,1:T(8,128)S(1)} %copy-done.6, f32[1024,4,128]{0,2,1:T(8,128)S(1)} %bitcast.99, f32[4]{0:T(128)S(1)} %get-tuple-element.227, f32[1024,4]{0,1:T(4,128)S(1)} %fusion.46, f32[4]{0:T(128)S(1)} %get-tuple-element.228, f32[4,128,128]{1,0,2:T(4,128)S(1)} %fusion.21), kind=kOutput, calls=%fused_computation.45 | convolution fusion | flops 807927808 | bytes 5521440 | tf_op jit(solution)/shard_map/thd,hde->the/dot_general | solution.py:121
  138.4 53.1 %all_to_all.21 = bf16[4,1024,512]{2,1,0:T(8,128)(2,1)S(1)} all-to-all(bf16[4,1024,512]{2,1,0:T(8,128)(2,1)S(1)} %broadcast_in_dim.67), channel_id=1, replica_groups=mesh['seq'=32,'head'=4] {'head'}, dimensions={0} | all-to-all | bytes 8388608 | tf_op jit(solution)/shard_map/all_to_all | solution.py:40
  191.5 8.0 %bitcast_convert_fusion = bf16[1024,1024]{1,0:T(8,128)(2,1)} fusion(bf16[512,4,1024]{2,0,1:T(8,128)(2,1)} %all-to-all-done.1, bf16[4,1024,512]{2,1,0:T(8,128)(2,1)S(1)} %all_to_all.21), kind=kOutput, calls=%fused_computation.25 | convolution fusion | flops 4296015872 | bytes 10485760 | tf_op jit(solution)/shard_map/dot_general | solution.py:150
  (74 shorter events, 19.2 us)
Async XLA Ops:
  6.5 30.7 %copy-start = (s32[64,2]{0,1:T(2,128)S(1)}, s32[64,2]{0,1:T(2,128)}, u32[]{:S(2)}) copy-start(s32[64,2]{0,1:T(2,128)} %param.12) | copy-start | bytes 1540
  6.5 1.6 copy-start.5
  6.5 121.1 %all-gather.2.cloned.1.call-start = ((), (), s32[]{:S(2)}) async-start(), calls=%async_computation.2 | async-start | bytes 8718336 | tf_op jit(solution)/shard_map/all_gather | solution.py:24
  11.7 31.8 %collective-permute-start.1 = (bf16[512,512]{0,1:T(8,128)(2,1)}, bf16[512,512]{0,1:T(8,128)(2,1)}, u32[]{:S(2)}, u32[]{:S(2)}) collective-permute-start(bf16[512,512]{0,1:T(8,128)(2,1)} %slice.27), channel_id=1, source_target_pairs={{0,4},{4,8},{8,12},{12,16},{16,20},{20,24},{24,28},{28,32},{32,36}... | collective-permute-start | bytes 1572872 | tf_op jit(solution)/shard_map/ppermute | solution.py:18
  14.1 11.3 %copy-start.3 = (bf16[1024,512]{0,1:T(8,128)(2,1)}, bf16[1024,512]{0,1:T(8,128)(2,1)S(1)}, u32[]{:S(2)}) copy-start(bf16[1024,512]{0,1:T(8,128)(2,1)S(1)} %copy.53) | copy-start | bytes 3145732
  15.0 31.2 %collective-permute-start = (bf16[512,512]{0,1:T(8,128)(2,1)}, bf16[512,512]{0,1:T(8,128)(2,1)}, u32[]{:S(2)}, u32[]{:S(2)}) collective-permute-start(bf16[512,512]{0,1:T(8,128)(2,1)} %slice.26), channel_id=1, source_target_pairs={{0,4},{4,8},{8,12},{12,16},{16,20},{20,24},{24,28},{28,32},{32,36}... | collective-permute-start | bytes 1572872 | tf_op jit(solution)/shard_map/ppermute | solution.py:18
  31.8 5.3 %copy-start.8 = (f32[32,4]{0,1:T(4,128)S(1)}, f32[32,4]{0,1:T(4,128)}, u32[]{:S(2)}) copy-start(f32[32,4]{0,1:T(4,128)} %param.13) | copy-start | bytes 1540
  31.8 106.3 %all-to-all-start.1 = ((bf16[512,4,1024]{2,0,1:T(8,128)(2,1)}), bf16[512,4,1024]{2,0,1:T(8,128)(2,1)}, u32[]{:S(2)}, u32[]{:S(2)}) async-start(bf16[512,4,1024]{2,0,1:T(8,128)(2,1)} %copy.63), calls=%async_computation.1 | async-start | bytes 8388608 | tf_op jit(solution)/shard_map/all_to_all | solution.py:149
  41.6 1.8 copy-start.9
  44.6 1.7 copy-start.4
  55.4 3.7 %copy-start.7 = (bf16[1536,4,128]{2,0,1:T(8,128)(2,1)S(1)}, bf16[1536,4,128]{2,0,1:T(8,128)(2,1)}, u32[]{:S(2)}) copy-start(bf16[1536,4,128]{2,0,1:T(8,128)(2,1)} %get-tuple-element.339) | copy-start | bytes 4718596 | tf_op jit(solution)/shard_map/while
  92.9 3.7 %copy-start.7 = (bf16[1536,4,128]{2,0,1:T(8,128)(2,1)S(1)}, bf16[1536,4,128]{2,0,1:T(8,128)(2,1)}, u32[]{:S(2)}) copy-start(bf16[1536,4,128]{2,0,1:T(8,128)(2,1)} %get-tuple-element.339) | copy-start | bytes 4718596 | tf_op jit(solution)/shard_map/while
  123.5 5.2 %copy-start.2 = (f32[1024,512]{0,1:T(8,128)S(1)}, f32[1024,512]{0,1:T(8,128)}, u32[]{:S(2)}) copy-start(f32[1024,512]{0,1:T(8,128)} %copy.84) | copy-start | bytes 6291460
  129.8 5.6 %copy-start.6 = (f32[1024,4,128]{0,2,1:T(8,128)S(1)}, f32[1024,4,128]{0,2,1:T(8,128)}, u32[]{:S(2)}) copy-start(f32[1024,4,128]{0,2,1:T(8,128)} %reshape.184) | copy-start | bytes 6291460
  191.5 8.0 %copy-start.1 = (s32[64,2]{0,1:T(2,128)S(1)}, s32[64,2]{0,1:T(2,128)}, u32[]{:S(2)}) copy-start(s32[64,2]{0,1:T(2,128)} %param.12) | copy-start | bytes 1540
Sparse Core Ops, SparseCore 0:
  10.9 56.4 all-gather.1
where the time goes:
time: 210 us; the launch traced here: 206 us
  local copies, waits for them, and re-layouts  75.6 us (36%)
  blocking collectives  53.1 us (25%)
  matrix products  30.7 us (15%)
  other arithmetic  20.8 us (10%)
  between operations  13.7 us (7%)
  starting transfers between devices  11.1 us (5%)
    all_to_all x1, blocking collectives, sent_to_all(): return lax.all_to_all(copies, axis, split_axis=0, concat_axis=0, tiled=True)  53.1 us
    dynamic_update_slice x4, local copies, waits for them, and re-layouts, local_attention(): blocks = lax.map(attend_block, jnp.arange(seg_rows // block_rows))  44 us
    unnamed x23, local copies, waits for them, and re-layouts  11.9 us
    dot_general x2, matrix products, attend_block(): jnp.einsum('hqk,khd->qhd', weights.astype(jnp.bfloat16), band_values, pre...  9.72 us
    dot_general x2, matrix products, attend_block(): jnp.einsum('qhd,khd->hqk', query_block, band_keys, preferred_element_type...  8.28 us
    dot_general x1, matrix products, body(): mixed = jnp.dot(gathered, columns, preferred_element_type=jnp.float32)  7.99 us
    reduce_sum x2, other arithmetic, attend_block(): totals = jnp.sum(weights, axis=-1)  7.29 us
    all_to_all x1, local copies, waits for them, and re-layouts, body(): lax.all_to_all(out_weight, 'head', split_axis=1, concat_axis=0, tiled=True)  6.32 us
  transfers between devices with their start and end apart: 4, of which 0 were waited for; matrix products, arithmetic and copies ran while one was open for 55% of the time, Pallas kernels for 0%

commit v1 on v0

v1 whole, which is shorter than its diff:
```python
import math

import jax
import jax.numpy as jnp
from jax import lax
from jax.experimental import pallas as pl
from jax.experimental.pallas import tpu as pltpu
from jax.sharding import PartitionSpec as P

SEG = 1024
BAND = 512
PART = 512
BLOCK = 256
HALF = 128
HEADS = 4
WIDTH = 128
COLS = 1024
GROUP = 4
ROW = 8
SLICE = 72
MESH = pl.DeviceIdType.MESH
EXPONENT = math.log2(math.e) / math.sqrt(WIDTH)
F32 = jnp.float32
BF16 = jnp.bfloat16


def feature_map(values_in):
    return jnp.where(values_in > 0, values_in + 1.0, jnp.exp(jnp.minimum(values_in, 0.0)))


def two_terms(values_in):
    high = values_in.astype(BF16)
    return high, (values_in - high.astype(F32)).astype(BF16)


def dot_last(a, b):
    return lax.dot_general(a, b, (((1,), (1,)), ((), ())), preferred_element_type=F32)


def dot_first(a, b):
    return lax.dot_general(a, b, (((0,), (0,)), ((), ())), preferred_element_type=F32)


def head_columns(head):
    return pl.ds(pl.multiple_of(head * WIDTH, WIDTH), WIDTH)


def kernel(
    spans, decay, gate, q_hbm, k_hbm, v_hbm, w_hbm, out_hbm,
    kbuf, vbuf, qbuf, gbuf, wbuf, obuf, local, bias, mem_high, mem_low,
    slices_out, slices_in, total_out, totals_in, mem_out, mem_in,
    load_sem, store_sem, band_s, band_r, wy_s, wy_r, wx_s, wx_r, wc_s, wc_r,
    a_s, a_r, b_s, b_r, c_s, c_r, g_s, g_r,
):
    seq = lax.axis_index("seq")
    head = lax.axis_index("head")
    x, place = seq // ROW, seq % ROW
    core, z = seq % 2, (seq % ROW) // 2
    n_seq = GROUP * ROW

    def along_y(d):
        return (seq, (head + d) % GROUP)

    def along_x(d):
        return (((x + d) % GROUP) * ROW + place, head)

    def along_row(d):
        return (x * ROW + (place + d) % ROW, head)

    partner = (seq + 1 - 2 * core, head)
    following, previous = ((seq + 1) % n_seq, head), ((seq + n_seq - 1) % n_seq, head)
    sent = []

    def remote(src, dst, send_sem, recv_sem, device):
        return pltpu.make_async_remote_copy(
            src_ref=src, dst_ref=dst, send_sem=send_sem, recv_sem=recv_sem,
            device_id=device, device_id_type=MESH,
        )

    def send(src, dst, send_sem, recv_sem, device):
        copy = remote(src, dst, send_sem, recv_sem, device)
        copy.start()
        sent.append(copy)

    def arrived(dst, send_sem, recv_sem, device):
        remote(dst, dst, send_sem, recv_sem, device).wait_recv()

    loads = [
        pltpu.make_async_copy(k_hbm, kbuf.at[pl.ds(BAND, SEG)], load_sem.at[0]),
        pltpu.make_async_copy(v_hbm, vbuf.at[pl.ds(BAND, SEG)], load_sem.at[1]),
        pltpu.make_async_copy(q_hbm, qbuf, load_sem.at[2]),
        pltpu.make_async_copy(
            w_hbm.at[:, pl.ds(pl.multiple_of(head * COLS, COLS), COLS)], wbuf.at[0], load_sem.at[3]
        ),
    ]
    for copy in loads:
        copy.start()

    barrier = pltpu.get_barrier_semaphore()
    sources = [along_y(d) for d in range(1, GROUP)] + [along_x(d) for d in range(1, GROUP)]
    sources += [along_row(d) for d in range(1, ROW)] + [previous]
    for device in sources:
        pl.semaphore_signal(barrier, inc=1, device_id=device, device_id_type=MESH)
    pl.semaphore_wait(barrier, len(sources))

    def piece_rows(d, of_core):
        return pl.ds(pl.multiple_of((((x + GROUP - d) % GROUP) * 2 + of_core) * 64, 64), 64)

    own_rows = piece_rows(0, core)
    for d in range(1, GROUP):
        send(
            w_hbm.at[own_rows, pl.ds(pl.multiple_of(((head + d) % GROUP) * COLS, COLS), COLS)],
            wbuf.at[GROUP - d, own_rows], wy_s.at[d], wy_r.at[d], along_y(d),
        )

    def band_pieces(which):
        for n in which:
            src, dst = (k_hbm, kbuf) if n < 4 else (v_hbm, vbuf)
            rows = (n % 4) * 128
            send(
                src.at[pl.ds(SEG - BAND + rows, 128)], dst.at[pl.ds(rows, 128)],
                band_s.at[n], band_r.at[n], following,
            )

    def band_arrived():
        for n in range(8):
            dst = kbuf if n < 4 else vbuf
            arrived(dst.at[pl.ds((n % 4) * 128, 128)], band_s.at[n], band_r.at[n], previous)

    band_pieces((0, 1))
    loads[0].wait()
    loads[1].wait()

    def state_of(h, carry):
        cols = head_columns(h)
        total = jnp.zeros((WIDTH, 2 * WIDTH), F32)
        sums = jnp.zeros((8, WIDTH), F32)
        for t in range(SEG // BLOCK):
            rows = pl.ds(BAND + t * BLOCK, BLOCK)
            feats = feature_map(kbuf[rows, cols].astype(F32))
            total += dot_first(vbuf[rows, cols], jnp.concatenate(two_terms(feats), axis=1))
            sums += jnp.sum(feats.reshape(BLOCK // 8, 8, WIDTH), axis=0)
        state = total[:, :WIDTH] + total[:, WIDTH:]
        sums = jnp.broadcast_to(jnp.sum(sums, axis=0, keepdims=True), (8, WIDTH))
        for half in range(2):
            slices_out[2 * h + half, :64] = state[64 * half : 64 * half + 64]
            slices_out[2 * h + half, 64:] = sums
        return carry

    lax.fori_loop(0, HEADS, state_of, 0)

    for d in range(1, ROW):
        send(
            slices_out.at[(place + d) % ROW], slices_in.at[place], a_s.at[d], a_r.at[d], along_row(d)
        )
    slices_in[place] = slices_out[place]
    band_pieces((2, 3, 4))
    loads[2].wait()

    def attend(part, sub):
        row = part * PART + sub * BLOCK
        count = 2 * PART - sub * BLOCK
        first = spans[0, 2 * seq + part] - seq * SEG
        last = spans[1, 2 * seq + part] - seq * SEG
        r = lax.broadcasted_iota(jnp.int32, (BLOCK, count), 0)
        j = lax.broadcasted_iota(jnp.int32, (BLOCK, count), 1)
        near = (j <= r + BAND) & (j > r)
        key_at, query_at = j + (row - BAND), r + row
        if part == 0:
            near = near & (key_at >= jnp.where(seq > 0, -BAND, 0))
        same = (query_at >= first) & (query_at < last) & (key_at >= first) & (key_at < last)
        bias[:, :count] = jnp.where(near | same, 0.0, -1e30)

        def one_head(h, carry):
            cols = head_columns(h)
            keys = kbuf[pl.ds(row, count), cols]
            scores = dot_last(qbuf[pl.ds(row, BLOCK), cols], keys) + bias[:, :count]
            weights = jnp.exp2((scores - jnp.max(scores, axis=1, keepdims=True)) * EXPONENT)
            mixed = jnp.dot(
                weights.astype(BF16), vbuf[pl.ds(row, count), cols], preferred_element_type=F32
            )
            local[pl.ds(row, BLOCK), cols] = mixed / jnp.sum(weights, axis=1, keepdims=True)
            return carry

        lax.fori_loop(0, HEADS, one_head, 0)

    attend(1, 0)

    for d in range(1, ROW):
        arrived(slices_in.at[(place + ROW - d) % ROW], a_s.at[d], a_r.at[d], along_row(ROW - d))
    total = slices_in[0]
    for t in range(1, ROW):
        total = decay[z, x * ROW + t] * total + slices_in[t]
    total_out[...] = total
    for d in range(1, GROUP):
        send(total_out, totals_in.at[x], b_s.at[d], b_r.at[d], along_x(d))
    totals_in[x] = total

    foreign = pl.ds(1, GROUP - 1)
    for d in range(1, GROUP):
        arrived(wbuf.at[GROUP - d, own_rows], wy_s.at[d], wy_r.at[d], along_y(GROUP - d))
    for d in range(1, GROUP):
        piece = wbuf.at[foreign, own_rows]
        send(piece, piece, wx_s.at[d], wx_r.at[d], along_x(d))
    send(wbuf.at[foreign, own_rows], wbuf.at[foreign, own_rows], wc_s.at[0], wc_r.at[0], partner)

    attend(1, 1)

    for d in range(1, GROUP):
        arrived(totals_in.at[(x + GROUP - d) % GROUP], b_s.at[d], b_r.at[d], along_x(GROUP - d))
    memory = jnp.zeros((SLICE, WIDTH), F32)
    for n in range(GROUP):
        product = decay[z, n * ROW]
        for t in range(1, ROW):
            product = product * decay[z, n * ROW + t]
        memory = jnp.where(n < x, product * memory + totals_in[n], memory)
    for t in range(ROW):
        mem_out[t] = memory
        memory = decay[z, x * ROW + t] * memory + slices_in[t]
    for d in range(1, ROW):
        send(mem_out.at[(place + d) % ROW], mem_in.at[place], c_s.at[d], c_r.at[d], along_row(d))
    mem_in[place] = mem_out[place]
    band_pieces((5, 6, 7))

    for d in range(1, ROW):
        arrived(mem_in.at[(place + ROW - d) % ROW], c_s.at[d], c_r.at[d], along_row(ROW - d))

    def place_memory(h, carry):
        norm = jnp.broadcast_to(mem_in[2 * h, 64:65], (WIDTH, WIDTH))
        both = jnp.concatenate([mem_in[2 * h, :64], mem_in[2 * h + 1, :64], norm], axis=0)
        high, low = two_terms(both)
        mem_high[h] = high
        mem_low[h] = low
        return carry

    lax.fori_loop(0, HEADS, place_memory, 0)

    def finish(row):
        def one_head(h, carry):
            cols = head_columns(h)
            high, low = two_terms(feature_map(qbuf[pl.ds(row, BLOCK), cols].astype(F32)))
            both = dot_last(high, mem_high[h]) + dot_last(high, mem_low[h]) + dot_last(low, mem_high[h])
            readout = both[:, :WIDTH] / (both[:, WIDTH:] + 1.0)
            mix = 1.0 / (1.0 + jnp.exp(-jnp.full((1, WIDTH), gate[h], F32)))
            mixed = mix * readout + (1.0 - mix) * local[pl.ds(row, BLOCK), cols]
            gbuf[0, pl.ds(row, BLOCK), cols] = mixed.astype(BF16)
            return carry

        lax.fori_loop(0, HEADS, one_head, 0)

    chunk_rows = (512, 768, 0, 256)

    def half_rows(chunk, half):
        return pl.ds(chunk_rows[chunk] + half * HALF, HALF)

    def share(chunk):
        for half in (0, 1):
            rows, at = half_rows(chunk, half), chunk * 6 + half
            send(gbuf.at[0, rows], gbuf.at[3, rows], g_s.at[at], g_r.at[at], along_y(1))
            rows, at = half_rows(chunk, 1 - half), chunk * 6 + 3 - half
            send(gbuf.at[0, rows], gbuf.at[1, rows], g_s.at[at], g_r.at[at], along_y(3))

    def relay(chunk):
        rows, at = half_rows(chunk, 0), chunk * 6
        arrived(gbuf.at[3, rows], g_s.at[at], g_r.at[at], along_y(3))
        send(gbuf.at[3, rows], gbuf.at[2, rows], g_s.at[at + 4], g_r.at[at + 4], along_y(1))
        rows = half_rows(chunk, 1)
        arrived(gbuf.at[1, rows], g_s.at[at + 3], g_r.at[at + 3], along_y(1))
        send(gbuf.at[1, rows], gbuf.at[2, rows], g_s.at[at + 5], g_r.at[at + 5], along_y(3))

    def gathered(chunk):
        at = chunk * 6
        arrived(gbuf.at[3, half_rows(chunk, 1)], g_s.at[at + 1], g_r.at[at + 1], along_y(3))
        arrived(gbuf.at[1, half_rows(chunk, 0)], g_s.at[at + 2], g_r.at[at + 2], along_y(1))
        arrived(gbuf.at[2, half_rows(chunk, 0)], g_s.at[at + 4], g_r.at[at + 4], along_y(3))
        arrived(gbuf.at[2, half_rows(chunk, 1)], g_s.at[at + 5], g_r.at[at + 5], along_y(1))

    stores = []

    def project(chunk):
        rows = pl.ds(chunk_rows[chunk], BLOCK)

        def one_tile(n, carry):
            cols = pl.ds(pl.multiple_of(n * 256, 256), 256)
            total = jnp.zeros((BLOCK, 256), F32)
            for j in range(GROUP):
                total += jnp.dot(gbuf[j, rows], wbuf[j, :, cols], preferred_element_type=F32)
            obuf[rows, cols] = total.astype(BF16)
            return carry

        lax.fori_loop(0, COLS // 256, one_tile, 0)
        copy = pltpu.make_async_copy(obuf.at[rows], out_hbm.at[rows], store_sem.at[chunk])
        copy.start()
        stores.append(copy)

    finish(512)
    share(0)
    finish(768)
    share(1)
    band_arrived()
    attend(0, 0)
    relay(0)
    finish(0)
    share(2)
    attend(0, 1)
    finish(256)
    share(3)
    relay(1)

    for d in range(1, GROUP):
        rows = piece_rows(d, core)
        arrived(wbuf.at[foreign, rows], wx_s.at[d], wx_r.at[d], along_x(GROUP - d))
        send(wbuf.at[foreign, rows], wbuf.at[foreign, rows], wc_s.at[d], wc_r.at[d], partner)
    for d in range(GROUP):
        arrived(wbuf.at[foreign, piece_rows(d, 1 - core)], wc_s.at[d], wc_r.at[d], partner)
    loads[3].wait()

    gathered(0)
    project(0)
    relay(2)
    gathered(1)
    project(1)
    relay(3)
    gathered(2)
    project(2)
    gathered(3)
    project(3)
    for copy in stores:
        copy.wait()
    for copy in sent:
        copy.wait_send()


def body(queries, keys, values, span_bounds, mem_decay, mem_gate, out_weight):
    smem = pl.BlockSpec(memory_space=pltpu.SMEM)
    anywhere = pl.BlockSpec(memory_space=pl.ANY)
    dma = pltpu.SemaphoreType.DMA
    return pl.pallas_call(
        kernel,
        out_shape=jax.ShapeDtypeStruct((SEG, COLS), BF16),
        in_specs=[smem, smem, smem, anywhere, anywhere, anywhere, anywhere],
        out_specs=anywhere,
        scratch_shapes=[
            pltpu.VMEM((BAND + SEG, HEADS * WIDTH), BF16),
            pltpu.VMEM((BAND + SEG, HEADS * WIDTH), BF16),
            pltpu.VMEM((SEG, HEADS * WIDTH), BF16),
            pltpu.VMEM((GROUP, SEG, HEADS * WIDTH), BF16),
            pltpu.VMEM((GROUP, HEADS * WIDTH, COLS), BF16),
            pltpu.VMEM((SEG, COLS), BF16),
            pltpu.VMEM((SEG, HEADS * WIDTH), F32),
            pltpu.VMEM((BLOCK, 2 * PART), F32),
            pltpu.VMEM((HEADS, 2 * WIDTH, WIDTH), BF16),
            pltpu.VMEM((HEADS, 2 * WIDTH, WIDTH), BF16),
            pltpu.VMEM((ROW, SLICE, WIDTH), F32),
            pltpu.VMEM((ROW, SLICE, WIDTH), F32),
            pltpu.VMEM((SLICE, WIDTH), F32),
            pltpu.VMEM((GROUP, SLICE, WIDTH), F32),
            pltpu.VMEM((ROW, SLICE, WIDTH), F32),
            pltpu.VMEM((ROW, SLICE, WIDTH), F32),
            dma((4,)), dma((4,)), dma((8,)), dma((8,)), dma((4,)), dma((4,)),
            dma((4,)), dma((4,)), dma((4,)), dma((4,)), dma((8,)), dma((8,)),
            dma((4,)), dma((4,)), dma((8,)), dma((8,)), dma((24,)), dma((24,)),
        ],
        compiler_params=pltpu.CompilerParams(
            collective_id=0, has_side_effects=True, vmem_limit_bytes=60 * 1024 * 1024
        ),
    )(span_bounds.T, mem_decay.T, mem_gate, queries, keys, values, out_weight)


def solution(mesh):
    return jax.shard_map(
        body,
        mesh=mesh,
        in_specs=(
            P("seq", "head"),
            P("seq", "head"),
            P("seq", "head"),
            P(),
            P(None, "head"),
            P("head"),
            P("head", None),
        ),
        out_specs=P("seq", "head"),
        check_vma=False,
    )
```

time: 210 us -> 79.7 us (0.38)
  the two profiles are of different devices: /device:TPU:4 before, /device:TPU:78 now
where the time goes in v1:
time: 79.7 us; the launch traced here: 79.5 us
  Pallas kernels  76.5 us (96%)
  local copies, waits for them, and re-layouts  3.08 us (4%)
    pallas_call x1, Pallas kernels, body(): pl.pallas_call(kernel, out_shape=jax.ShapeDtypeStruct((SEG, COLS), BF16),...  76.5 us
    unnamed x1, local copies, waits for them, and re-layouts  3.08 us

profile of v1, /device:TPU:78, one launch (start us, length us, event | category | flops | bytes accessed | tf_op | source)
XLA Modules:
  0.0 79.5 jit_solution(3024843141871258144)
XLA Ops:
  0.0 76.5 %shard_map.73 = bf16[1024,1024]{1,0:T(8,128)(2,1)} custom-call(s32[2,64]{1,0:T(2,128)} %bitcast.3, f32[4,32]{1,0:T(4,128)} %bitcast.2, f32[4]{0:T(128)} %gate.1, bf16[1024,512]{1,0:T(8,128)(2,1)} %q_hbm.1, bf16[1024,512]{1,0:T(8,128)(2,1)} %k_hbm.1, bf16[1024,512]{1,0:T(8,128)(2,1)} %v_hbm.1, bf16[512,4096]{1,0:T(8,128)(2,1)} %w_hbm.1), custom_call_target="tpu_custom_call" | custom-call | tf_op jit(solution)/shard_map/pallas_call | solution.py:338
  76.5 3.1 %copy.9 = bf16[1024,1024]{1,0:T(8,128)(2,1)} copy(bf16[1024,1024]{1,0:T(8,128)(2,1)} %shard_map.73) | data formatting | bytes 4194304

commit v2 on v1

--- a/solution.py
+++ b/solution.py
@@ -47,7 +47,7 @@
 
 def kernel(
     spans, decay, gate, q_hbm, k_hbm, v_hbm, w_hbm, out_hbm,
-    kbuf, vbuf, qbuf, gbuf, wbuf, obuf, local, bias, mem_high, mem_low,
+    kbuf, vbuf, qbuf, gbuf, wbuf, obuf, local, bias, mem,
     slices_out, slices_in, total_out, totals_in, mem_out, mem_in,
     load_sem, store_sem, band_s, band_r, wy_s, wy_r, wx_s, wx_r, wc_s, wc_r,
     a_s, a_r, b_s, b_r, c_s, c_r, g_s, g_r,
@@ -93,43 +93,33 @@
             w_hbm.at[:, pl.ds(pl.multiple_of(head * COLS, COLS), COLS)], wbuf.at[0], load_sem.at[3]
         ),
     ]
-    for copy in loads:
-        copy.start()
+    loads[0].start()
+    loads[1].start()
 
     barrier = pltpu.get_barrier_semaphore()
     sources = [along_y(d) for d in range(1, GROUP)] + [along_x(d) for d in range(1, GROUP)]
     sources += [along_row(d) for d in range(1, ROW)] + [previous]
     for device in sources:
         pl.semaphore_signal(barrier, inc=1, device_id=device, device_id_type=MESH)
-    pl.semaphore_wait(barrier, len(sources))
 
     def piece_rows(d, of_core):
         return pl.ds(pl.multiple_of((((x + GROUP - d) % GROUP) * 2 + of_core) * 64, 64), 64)
 
     own_rows = piece_rows(0, core)
-    for d in range(1, GROUP):
-        send(
-            w_hbm.at[own_rows, pl.ds(pl.multiple_of(((head + d) % GROUP) * COLS, COLS), COLS)],
-            wbuf.at[GROUP - d, own_rows], wy_s.at[d], wy_r.at[d], along_y(d),
-        )
-
-    def band_pieces(which):
-        for n in which:
-            src, dst = (k_hbm, kbuf) if n < 4 else (v_hbm, vbuf)
-            rows = (n % 4) * 128
-            send(
-                src.at[pl.ds(SEG - BAND + rows, 128)], dst.at[pl.ds(rows, 128)],
-                band_s.at[n], band_r.at[n], following,
-            )
-
-    def band_arrived():
-        for n in range(8):
-            dst = kbuf if n < 4 else vbuf
-            arrived(dst.at[pl.ds((n % 4) * 128, 128)], band_s.at[n], band_r.at[n], previous)
-
-    band_pieces((0, 1))
+
+    def band_piece(n):
+        hbm, ref = (k_hbm, kbuf) if n % 2 == 0 else (v_hbm, vbuf)
+        rows = BLOCK - (n // 2) * BLOCK
+        return hbm.at[pl.ds(SEG - BAND + rows, BLOCK)], ref.at[pl.ds(rows, BLOCK)]
+
+    def band_arrived(half):
+        for n in (2 * half, 2 * half + 1):
+            arrived(band_piece(n)[1], band_s.at[n], band_r.at[n], previous)
+
     loads[0].wait()
     loads[1].wait()
+    loads[2].start()
+    loads[3].start()
 
     def state_of(h, carry):
         cols = head_columns(h)
@@ -141,20 +131,25 @@
             total += dot_first(vbuf[rows, cols], jnp.concatenate(two_terms(feats), axis=1))
             sums += jnp.sum(feats.reshape(BLOCK // 8, 8, WIDTH), axis=0)
         state = total[:, :WIDTH] + total[:, WIDTH:]
-        sums = jnp.broadcast_to(jnp.sum(sums, axis=0, keepdims=True), (8, WIDTH))
+        sums = jnp.broadcast_to(jnp.sum(sums, axis=0, keepdims=True), (8, WIDTH)).astype(BF16)
         for half in range(2):
-            slices_out[2 * h + half, :64] = state[64 * half : 64 * half + 64]
+            slices_out[2 * h + half, :64] = state[64 * half : 64 * half + 64].astype(BF16)
             slices_out[2 * h + half, 64:] = sums
         return carry
 
     lax.fori_loop(0, HEADS, state_of, 0)
 
+    pl.semaphore_wait(barrier, len(sources))
     for d in range(1, ROW):
         send(
             slices_out.at[(place + d) % ROW], slices_in.at[place], a_s.at[d], a_r.at[d], along_row(d)
         )
     slices_in[place] = slices_out[place]
-    band_pieces((2, 3, 4))
+    for d in range(1, GROUP):
+        send(
+            w_hbm.at[own_rows, pl.ds(pl.multiple_of(((head + d) % GROUP) * COLS, COLS), COLS)],
+            wbuf.at[GROUP - d, own_rows], wy_s.at[d], wy_r.at[d], along_y(d),
+        )
     loads[2].wait()
 
     def attend(part, sub):
@@ -188,21 +183,13 @@
 
     for d in range(1, ROW):
         arrived(slices_in.at[(place + ROW - d) % ROW], a_s.at[d], a_r.at[d], along_row(ROW - d))
-    total = slices_in[0]
+    total = slices_in[0].astype(F32)
     for t in range(1, ROW):
-        total = decay[z, x * ROW + t] * total + slices_in[t]
-    total_out[...] = total
+        total = decay[z, x * ROW + t] * total + slices_in[t].astype(F32)
+    total_out[...] = total.astype(BF16)
     for d in range(1, GROUP):
         send(total_out, totals_in.at[x], b_s.at[d], b_r.at[d], along_x(d))
-    totals_in[x] = total
-
-    foreign = pl.ds(1, GROUP - 1)
-    for d in range(1, GROUP):
-        arrived(wbuf.at[GROUP - d, own_rows], wy_s.at[d], wy_r.at[d], along_y(GROUP - d))
-    for d in range(1, GROUP):
-        piece = wbuf.at[foreign, own_rows]
-        send(piece, piece, wx_s.at[d], wx_r.at[d], along_x(d))
-    send(wbuf.at[foreign, own_rows], wbuf.at[foreign, own_rows], wc_s.at[0], wc_r.at[0], partner)
+    totals_in[x] = total_out[...]
 
     attend(1, 1)
 
@@ -213,52 +200,78 @@
         product = decay[z, n * ROW]
         for t in range(1, ROW):
             product = product * decay[z, n * ROW + t]
-        memory = jnp.where(n < x, product * memory + totals_in[n], memory)
+        memory = jnp.where(n < x, product * memory + totals_in[n].astype(F32), memory)
     for t in range(ROW):
-        mem_out[t] = memory
-        memory = decay[z, x * ROW + t] * memory + slices_in[t]
+        mem_out[t] = memory.astype(BF16)
+        memory = decay[z, x * ROW + t] * memory + slices_in[t].astype(F32)
     for d in range(1, ROW):
         send(mem_out.at[(place + d) % ROW], mem_in.at[place], c_s.at[d], c_r.at[d], along_row(d))
     mem_in[place] = mem_out[place]
-    band_pieces((5, 6, 7))
+    foreign = pl.ds(1, GROUP - 1)
+    for d in range(1, GROUP):
+        arrived(wbuf.at[GROUP - d, own_rows], wy_s.at[d], wy_r.at[d], along_y(GROUP - d))
+
+    def pass_weights(d, half, at, device):
+        piece = weight_half(d, half)
+        send(piece, piece, wx_s.at[at], wx_r.at[at], device)
+
+    def weight_half(d, half):
+        row = (((x + GROUP - d) % GROUP) * 2 + core) * 64 + 32 * half
+        return wbuf.at[foreign, pl.ds(pl.multiple_of(row, 32), 32)]
+
+    def weights_in(d, half, at, device):
+        arrived(weight_half(d, half), wx_s.at[at], wx_r.at[at], device)
+
+    for half in (0, 1):
+        pass_weights(0, half, half, along_x(1))
+        pass_weights(0, 1 - half, 3 - half, along_x(3))
+    send(wbuf.at[foreign, own_rows], wbuf.at[foreign, own_rows], wc_s.at[0], wc_r.at[0], partner)
 
     for d in range(1, ROW):
         arrived(mem_in.at[(place + ROW - d) % ROW], c_s.at[d], c_r.at[d], along_row(ROW - d))
 
+    for n in range(4):
+        send(*band_piece(n), band_s.at[n], band_r.at[n], following)
+
     def place_memory(h, carry):
-        norm = jnp.broadcast_to(mem_in[2 * h, 64:65], (WIDTH, WIDTH))
-        both = jnp.concatenate([mem_in[2 * h, :64], mem_in[2 * h + 1, :64], norm], axis=0)
-        high, low = two_terms(both)
-        mem_high[h] = high
-        mem_low[h] = low
+        mem[h, :64] = mem_in[2 * h, :64]
+        mem[h, 64:WIDTH] = mem_in[2 * h + 1, :64]
+        mem[h, WIDTH:] = jnp.broadcast_to(mem_in[2 * h, 64:65], (WIDTH, WIDTH))
         return carry
 
     lax.fori_loop(0, HEADS, place_memory, 0)
 
-    def finish(row):
+    def finish(row, count):
         def one_head(h, carry):
             cols = head_columns(h)
-            high, low = two_terms(feature_map(qbuf[pl.ds(row, BLOCK), cols].astype(F32)))
-            both = dot_last(high, mem_high[h]) + dot_last(high, mem_low[h]) + dot_last(low, mem_high[h])
+            high, low = two_terms(feature_map(qbuf[pl.ds(row, count), cols].astype(F32)))
+            both = dot_last(high, mem[h]) + dot_last(low, mem[h])
             readout = both[:, :WIDTH] / (both[:, WIDTH:] + 1.0)
             mix = 1.0 / (1.0 + jnp.exp(-jnp.full((1, WIDTH), gate[h], F32)))
-            mixed = mix * readout + (1.0 - mix) * local[pl.ds(row, BLOCK), cols]
-            gbuf[0, pl.ds(row, BLOCK), cols] = mixed.astype(BF16)
+            mixed = mix * readout + (1.0 - mix) * local[pl.ds(row, count), cols]
+            gbuf[0, pl.ds(row, count), cols] = mixed.astype(BF16)
             return carry
 
-        lax.fori_loop(0, HEADS, one_head, 0)
-
-    chunk_rows = (512, 768, 0, 256)
+        lax.fori_loop(0, HEADS, one_head, 0, unroll=True)
+
+    chunk_rows = (512, 768, 256, 0)
 
     def half_rows(chunk, half):
         return pl.ds(chunk_rows[chunk] + half * HALF, HALF)
 
+    def to_right(chunk, half):
+        rows, at = half_rows(chunk, half), chunk * 6 + half
+        send(gbuf.at[0, rows], gbuf.at[3, rows], g_s.at[at], g_r.at[at], along_y(1))
+
+    def to_left(chunk, half):
+        rows, at = half_rows(chunk, half), chunk * 6 + 2 + half
+        send(gbuf.at[0, rows], gbuf.at[1, rows], g_s.at[at], g_r.at[at], along_y(3))
+
     def share(chunk):
-        for half in (0, 1):
-            rows, at = half_rows(chunk, half), chunk * 6 + half
-            send(gbuf.at[0, rows], gbuf.at[3, rows], g_s.at[at], g_r.at[at], along_y(1))
-            rows, at = half_rows(chunk, 1 - half), chunk * 6 + 3 - half
-            send(gbuf.at[0, rows], gbuf.at[1, rows], g_s.at[at], g_r.at[at], along_y(3))
+        to_right(chunk, 0)
+        to_left(chunk, 1)
+        to_right(chunk, 1)
+        to_left(chunk, 0)
 
     def relay(chunk):
         rows, at = half_rows(chunk, 0), chunk * 6
@@ -268,63 +281,112 @@
         arrived(gbuf.at[1, rows], g_s.at[at + 3], g_r.at[at + 3], along_y(1))
         send(gbuf.at[1, rows], gbuf.at[2, rows], g_s.at[at + 5], g_r.at[at + 5], along_y(3))
 
-    def gathered(chunk):
+    def adjacent(chunk):
         at = chunk * 6
         arrived(gbuf.at[3, half_rows(chunk, 1)], g_s.at[at + 1], g_r.at[at + 1], along_y(3))
         arrived(gbuf.at[1, half_rows(chunk, 0)], g_s.at[at + 2], g_r.at[at + 2], along_y(1))
+
+    def opposite(chunk):
+        at = chunk * 6
         arrived(gbuf.at[2, half_rows(chunk, 0)], g_s.at[at + 4], g_r.at[at + 4], along_y(3))
         arrived(gbuf.at[2, half_rows(chunk, 1)], g_s.at[at + 5], g_r.at[at + 5], along_y(1))
 
     stores = []
 
-    def project(chunk):
+    def product(rows, cols, owners):
+        total = jnp.dot(gbuf[owners[0], rows], wbuf[owners[0], :, cols], preferred_element_type=F32)
+        for j in owners[1:]:
+            total += jnp.dot(gbuf[j, rows], wbuf[j, :, cols], preferred_element_type=F32)
+        return total
+
+    def tiles(one_tile):
+        def step(n, carry):
+            one_tile(pl.ds(pl.multiple_of(n * 256, 256), 256))
+            return carry
+
+        lax.fori_loop(0, COLS // 256, step, 0)
+
+    def store(chunk):
         rows = pl.ds(chunk_rows[chunk], BLOCK)
-
-        def one_tile(n, carry):
-            cols = pl.ds(pl.multiple_of(n * 256, 256), 256)
-            total = jnp.zeros((BLOCK, 256), F32)
-            for j in range(GROUP):
-                total += jnp.dot(gbuf[j, rows], wbuf[j, :, cols], preferred_element_type=F32)
-            obuf[rows, cols] = total.astype(BF16)
-            return carry
-
-        lax.fori_loop(0, COLS // 256, one_tile, 0)
         copy = pltpu.make_async_copy(obuf.at[rows], out_hbm.at[rows], store_sem.at[chunk])
         copy.start()
         stores.append(copy)
 
-    finish(512)
-    share(0)
-    finish(768)
+    def project(chunk):
+        rows = pl.ds(chunk_rows[chunk], BLOCK)
+
+        def one_tile(cols):
+            obuf[rows, cols] = product(rows, cols, (0, 1, 2, 3)).astype(BF16)
+
+        tiles(one_tile)
+        store(chunk)
+
+    def project_near(chunk):
+        rows = pl.ds(chunk_rows[chunk], BLOCK)
+
+        def one_tile(cols):
+            bias[:, cols] = product(rows, cols, (0, 1, 3))
+
+        tiles(one_tile)
+
+    def project_far(chunk):
+        rows = pl.ds(chunk_rows[chunk], BLOCK)
+
+        def one_tile(cols):
+            obuf[rows, cols] = (bias[:, cols] + product(rows, cols, (2,))).astype(BF16)
+
+        tiles(one_tile)
+        store(chunk)
+
+    finish(512, HALF)
+    to_right(0, 0)
+    to_left(0, 0)
+    finish(512 + HALF, HALF)
+    to_right(0, 1)
+    to_left(0, 1)
+    finish(768, BLOCK)
     share(1)
-    band_arrived()
+    weights_in(1, 0, 0, along_x(3))
+    pass_weights(1, 0, 4, along_x(1))
+    weights_in(3, 1, 3, along_x(1))
+    pass_weights(3, 1, 5, along_x(3))
+    band_arrived(0)
+    attend(0, 1)
+    relay(0)
+    finish(256, BLOCK)
+    share(2)
+    relay(1)
+    band_arrived(1)
     attend(0, 0)
-    relay(0)
-    finish(0)
-    share(2)
-    attend(0, 1)
-    finish(256)
+    finish(0, BLOCK)
     share(3)
-    relay(1)
-
+
+    weights_in(1, 1, 1, along_x(3))
+    weights_in(3, 0, 2, along_x(1))
+    weights_in(2, 0, 4, along_x(3))
+    weights_in(2, 1, 5, along_x(1))
     for d in range(1, GROUP):
         rows = piece_rows(d, core)
-        arrived(wbuf.at[foreign, rows], wx_s.at[d], wx_r.at[d], along_x(GROUP - d))
         send(wbuf.at[foreign, rows], wbuf.at[foreign, rows], wc_s.at[d], wc_r.at[d], partner)
     for d in range(GROUP):
         arrived(wbuf.at[foreign, piece_rows(d, 1 - core)], wc_s.at[d], wc_r.at[d], partner)
     loads[3].wait()
 
-    gathered(0)
+    adjacent(0)
+    opposite(0)
     project(0)
     relay(2)
-    gathered(1)
+    adjacent(1)
+    opposite(1)
     project(1)
     relay(3)
-    gathered(2)
+    adjacent(2)
+    opposite(2)
     project(2)
-    gathered(3)
-    project(3)
+    adjacent(3)
+    project_near(3)
+    opposite(3)
+    project_far(3)
     for copy in stores:
         copy.wait()
     for copy in sent:
@@ -350,15 +412,14 @@
             pltpu.VMEM((SEG, HEADS * WIDTH), F32),
             pltpu.VMEM((BLOCK, 2 * PART), F32),
             pltpu.VMEM((HEADS, 2 * WIDTH, WIDTH), BF16),
-            pltpu.VMEM((HEADS, 2 * WIDTH, WIDTH), BF16),
-            pltpu.VMEM((ROW, SLICE, WIDTH), F32),
-            pltpu.VMEM((ROW, SLICE, WIDTH), F32),
-            pltpu.VMEM((SLICE, WIDTH), F32),
-            pltpu.VMEM((GROUP, SLICE, WIDTH), F32),
-            pltpu.VMEM((ROW, SLICE, WIDTH), F32),
-            pltpu.VMEM((ROW, SLICE, WIDTH), F32),
-            dma((4,)), dma((4,)), dma((8,)), dma((8,)), dma((4,)), dma((4,)),
-            dma((4,)), dma((4,)), dma((4,)), dma((4,)), dma((8,)), dma((8,)),
+            pltpu.VMEM((ROW, SLICE, WIDTH), BF16),
+            pltpu.VMEM((ROW, SLICE, WIDTH), BF16),
+            pltpu.VMEM((SLICE, WIDTH), BF16),
+            pltpu.VMEM((GROUP, SLICE, WIDTH), BF16),
+            pltpu.VMEM((ROW, SLICE, WIDTH), BF16),
+            pltpu.VMEM((ROW, SLICE, WIDTH), BF16),
+            dma((4,)), dma((4,)), dma((4,)), dma((4,)), dma((4,)), dma((4,)),
+            dma((6,)), dma((6,)), dma((4,)), dma((4,)), dma((8,)), dma((8,)),
             dma((4,)), dma((4,)), dma((8,)), dma((8,)), dma((24,)), dma((24,)),
         ],
         compiler_params=pltpu.CompilerParams(

time: 79.7 us -> 64.3 us (0.81)
  the two profiles are of different devices: /device:TPU:78 before, /device:TPU:0 now
where the time goes in v2:
time: 64.3 us; the launch traced here: 64.1 us
  Pallas kernels  61 us (95%)
  local copies, waits for them, and re-layouts  3.08 us (5%)
    pallas_call x1, Pallas kernels, body(): pl.pallas_call(kernel, out_shape=jax.ShapeDtypeStruct((SEG, COLS), BF16),...  61 us
    unnamed x1, local copies, waits for them, and re-layouts  3.08 us

profile of v2, /device:TPU:0, one launch (start us, length us, event | category | flops | bytes accessed | tf_op | source)
XLA Modules:
  0.0 64.1 jit_solution(11821803894185351715)
XLA Ops:
  0.0 61.0 %shard_map.73 = bf16[1024,1024]{1,0:T(8,128)(2,1)} custom-call(s32[2,64]{1,0:T(2,128)} %bitcast.3, f32[4,32]{1,0:T(4,128)} %bitcast.2, f32[4]{0:T(128)} %gate.1, bf16[1024,512]{1,0:T(8,128)(2,1)} %q_hbm.1, bf16[1024,512]{1,0:T(8,128)(2,1)} %k_hbm.1, bf16[1024,512]{1,0:T(8,128)(2,1)} %v_hbm.1, bf16[512,4096]{1,0:T(8,128)(2,1)} %w_hbm.1), custom_call_target="tpu_custom_call" | custom-call | tf_op jit(solution)/shard_map/pallas_call | solution.py:400
  61.0 3.1 %copy.9 = bf16[1024,1024]{1,0:T(8,128)(2,1)} copy(bf16[1024,1024]{1,0:T(8,128)(2,1)} %shard_map.73) | data formatting | bytes 4194304

commit v3 on v2

v3 whole, which is shorter than its diff:
```python
import functools
import math

import jax
import jax.numpy as jnp
from jax import lax
from jax.experimental import pallas as pl
from jax.experimental.pallas import tpu as pltpu
from jax.sharding import PartitionSpec as P

SEG = 1024
BAND = 512
PART = 512
BLOCK = 256
HALF = 128
HEADS = 4
WIDTH = 128
COLS = 1024
GROUP = 4
ROW = 8
SLICE = 72
MESH = pl.DeviceIdType.MESH
EXPONENT = math.log2(math.e) / math.sqrt(WIDTH)
F32 = jnp.float32
BF16 = jnp.bfloat16


def feature_map(values_in):
    return jnp.where(values_in > 0, values_in + 1.0, jnp.exp(jnp.minimum(values_in, 0.0)))


def two_terms(values_in):
    high = values_in.astype(BF16)
    return high, (values_in - high.astype(F32)).astype(BF16)


def dot_last(a, b):
    return lax.dot_general(a, b, (((1,), (1,)), ((), ())), preferred_element_type=F32)


def dot_first(a, b):
    return lax.dot_general(a, b, (((0,), (0,)), ((), ())), preferred_element_type=F32)


def head_columns(head):
    return pl.ds(pl.multiple_of(head * WIDTH, WIDTH), WIDTH)


def kernel(
    spans_hbm, decay_hbm, gate_hbm, q_hbm, k_hbm, v_hbm, w_hbm, out,
    spans, decay, gate, kbuf, vbuf, qbuf, gbuf, wbuf, local, bias, near_sum, mem, state_sum, key_sum,
    slices_out, slices_in, total_out, totals_in, mem_out, mem_in,
    load_sem, small_sem, send_sem, b_s, b_r, recv_sem, w_r, band_r, g_r,
):
    seq = lax.axis_index("seq")
    head = lax.axis_index("head")
    x, place = seq // ROW, seq % ROW
    core, z = seq % 2, (seq % ROW) // 2
    n_seq = GROUP * ROW

    def along_y(d):
        return (seq, (head + d) % GROUP)

    def along_x(d):
        return (((x + d) % GROUP) * ROW + place, head)

    def along_row(d):
        return (x * ROW + (place + d) % ROW, head)

    partner = (seq + 1 - 2 * core, head)
    following, previous = ((seq + 1) % n_seq, head), ((seq + n_seq - 1) % n_seq, head)
    state_sent, mem_sent, wy_sent, wx_sent, wc_sent, band_sent, g_sent = (send_sem.at[n] for n in range(7))

    def send(src, dst, send_sem, recv_sem, device):
        pltpu.make_async_remote_copy(
            src_ref=src, dst_ref=dst, send_sem=send_sem, recv_sem=recv_sem,
            device_id=device, device_id_type=MESH,
        ).start()

    def wait_bytes(like, sem):
        pltpu.make_async_copy(like, like, sem).wait()

    small = [
        pltpu.make_async_copy(src, dst, small_sem.at[n])
        for n, (src, dst) in enumerate(((spans_hbm, spans), (decay_hbm, decay), (gate_hbm, gate)))
    ]
    loads = []
    for t in range(SEG // BLOCK):
        for hbm, ref in ((k_hbm, kbuf), (v_hbm, vbuf)):
            copy = pltpu.make_async_copy(
                hbm.at[pl.ds(t * BLOCK, BLOCK)], ref.at[pl.ds(BAND + t * BLOCK, BLOCK)],
                load_sem.at[len(loads)],
            )
            copy.start()
            loads.append(copy)
    load_q = pltpu.make_async_copy(q_hbm, qbuf, load_sem.at[8])
    load_w = pltpu.make_async_copy(
        w_hbm.at[:, pl.ds(pl.multiple_of(head * COLS, COLS), COLS)], wbuf.at[0], load_sem.at[9]
    )

    barrier = pltpu.get_barrier_semaphore()
    sources = [along_y(d) for d in range(1, GROUP)] + [along_x(d) for d in range(1, GROUP)]
    sources += [along_row(d) for d in range(1, ROW)] + [previous]
    for device in sources:
        pl.semaphore_signal(barrier, inc=1, device_id=device, device_id_type=MESH)

    def piece_rows(d, of_core):
        return pl.ds(pl.multiple_of((((x + GROUP - d) % GROUP) * 2 + of_core) * 64, 64), 64)

    own_rows = piece_rows(0, core)

    def band_piece(n):
        hbm, ref = (k_hbm, kbuf) if n % 2 == 0 else (v_hbm, vbuf)
        rows = BLOCK - (n // 2) * BLOCK
        return hbm.at[pl.ds(SEG - BAND + rows, BLOCK)], ref.at[pl.ds(rows, BLOCK)]

    def band_arrived(half):
        wait_bytes(kbuf.at[pl.ds(0, 2 * BLOCK)], band_r.at[half])

    state_sum[...] = jnp.zeros((HEADS, WIDTH, 2 * WIDTH), F32)
    key_sum[...] = jnp.zeros((HEADS, 8, WIDTH), F32)
    for t in range(SEG // BLOCK):
        loads[2 * t].wait()
        loads[2 * t + 1].wait()
        rows = pl.ds(BAND + t * BLOCK, BLOCK)
        for h in range(HEADS):
            cols = pl.ds(h * WIDTH, WIDTH)
            feats = feature_map(kbuf[rows, cols].astype(F32))
            state_sum[h] += dot_first(vbuf[rows, cols], jnp.concatenate(two_terms(feats), axis=1))
            key_sum[h] += jnp.sum(feats.reshape(BLOCK // 8, 8, WIDTH), axis=0)
    load_q.start()
    load_w.start()
    for copy in small:
        copy.start()
    for h in range(HEADS):
        state = (state_sum[h, :, :WIDTH] + state_sum[h, :, WIDTH:]).astype(BF16)
        sums = jnp.sum(key_sum[h], axis=0, keepdims=True)
        for half in range(2):
            slices_out[2 * h + half, :64] = state[64 * half : 64 * half + 64]
            slices_out[2 * h + half, 64:] = jnp.broadcast_to(sums, (8, WIDTH)).astype(BF16)

    pl.semaphore_wait(barrier, len(sources))
    for d in range(1, ROW):
        send(
            slices_out.at[(place + d) % ROW], slices_in.at[place], state_sent, recv_sem.at[0], along_row(d)
        )
    slices_in[place] = slices_out[place]
    for d in range(1, GROUP):
        send(
            w_hbm.at[own_rows, pl.ds(pl.multiple_of(((head + d) % GROUP) * COLS, COLS), COLS)],
            wbuf.at[GROUP - d, own_rows], wy_sent, w_r.at[0], along_y(d),
        )
    for copy in small:
        copy.wait()
    load_q.wait()

    def attend(part, sub):
        row = part * PART + sub * BLOCK
        count = 2 * PART - sub * BLOCK
        first = spans[0, 2 * seq + part] - seq * SEG
        last = spans[1, 2 * seq + part] - seq * SEG
        r = lax.broadcasted_iota(jnp.int32, (BLOCK, count), 0)
        j = lax.broadcasted_iota(jnp.int32, (BLOCK, count), 1)
        near = (j <= r + BAND) & (j > r)
        key_at, query_at = j + (row - BAND), r + row
        if part == 0:
            near = near & (key_at >= jnp.where(seq > 0, -BAND, 0))
        same = (query_at >= first) & (query_at < last) & (key_at >= first) & (key_at < last)
        bias[:, :count] = jnp.where(near | same, 0.0, -1e30)

        def one_head(h, carry):
            cols = head_columns(h)
            keys = kbuf[pl.ds(row, count), cols]
            scores = dot_last(qbuf[pl.ds(row, BLOCK), cols], keys) + bias[:, :count]
            weights = jnp.exp2((scores - jnp.max(scores, axis=1, keepdims=True)) * EXPONENT)
            mixed = jnp.dot(
                weights.astype(BF16), vbuf[pl.ds(row, count), cols], preferred_element_type=F32
            )
            local[pl.ds(row, BLOCK), cols] = mixed / jnp.sum(weights, axis=1, keepdims=True)
            return carry

        lax.fori_loop(0, HEADS, one_head, 0)

    attend(1, 0)

    wait_bytes(slices_in.at[pl.ds(0, ROW - 1)], recv_sem.at[0])
    total = slices_in[0].astype(F32)
    for t in range(1, ROW):
        total = decay[z, x * ROW + t] * total + slices_in[t].astype(F32)
    total_out[...] = total.astype(BF16)

    def total_copy(d):
        return pltpu.make_async_remote_copy(
            src_ref=total_out, dst_ref=totals_in.at[x], send_sem=b_s.at[d], recv_sem=b_r.at[d],
            device_id=along_x(d), device_id_type=MESH,
        )

    for d in range(1, GROUP):
        pl.when(x + d < GROUP)(total_copy(d).start)

    attend(1, 1)

    for d in range(1, GROUP):
        pl.when(x >= d)(functools.partial(wait_bytes, total_out, b_r.at[d]))
    memory = jnp.zeros((SLICE, WIDTH), F32)
    for n in range(GROUP):
        product = decay[z, n * ROW]
        for t in range(1, ROW):
            product = product * decay[z, n * ROW + t]
        memory = jnp.where(n < x, product * memory + totals_in[n].astype(F32), memory)
    for t in range(ROW):
        mem_out[t] = memory.astype(BF16)
        memory = decay[z, x * ROW + t] * memory + slices_in[t].astype(F32)
    for d in range(1, ROW):
        send(mem_out.at[(place + d) % ROW], mem_in.at[place], mem_sent, recv_sem.at[1], along_row(d))
    mem_in[place] = mem_out[place]
    foreign = pl.ds(1, GROUP - 1)
    wait_bytes(wbuf.at[foreign, own_rows], w_r.at[0])

    def pass_weights(d, half, at, device):
        piece = weight_half(d, half)
        send(piece, piece, wx_sent, w_r.at[at], device)

    def weight_half(d, half):
        row = (((x + GROUP - d) % GROUP) * 2 + core) * 64 + 32 * half
        return wbuf.at[foreign, pl.ds(pl.multiple_of(row, 32), 32)]

    for half in (0, 1):
        pass_weights(0, half, (1, 3)[half], along_x(1))
        pass_weights(0, 1 - half, (2, 3)[half], along_x(3))
    send(wbuf.at[foreign, own_rows], wbuf.at[foreign, own_rows], wc_sent, w_r.at[4], partner)

    wait_bytes(mem_in.at[pl.ds(0, ROW - 1)], recv_sem.at[1])

    for n in range(4):
        send(*band_piece(n), band_sent, band_r.at[n // 2], following)

    def place_memory(h, carry):
        mem[h, :64] = mem_in[2 * h, :64]
        mem[h, 64:WIDTH] = mem_in[2 * h + 1, :64]
        mem[h, WIDTH:] = jnp.broadcast_to(mem_in[2 * h, 64:65], (WIDTH, WIDTH))
        return carry

    lax.fori_loop(0, HEADS, place_memory, 0)

    def finish(row, count):
        def one_head(h, carry):
            cols = head_columns(h)
            high, low = two_terms(feature_map(qbuf[pl.ds(row, count), cols].astype(F32)))
            both = dot_last(high, mem[h]) + dot_last(low, mem[h])
            readout = both[:, :WIDTH] / (both[:, WIDTH:] + 1.0)
            mix = 1.0 / (1.0 + jnp.exp(-jnp.full((1, WIDTH), gate[h], F32)))
            mixed = mix * readout + (1.0 - mix) * local[pl.ds(row, count), cols]
            gbuf[0, pl.ds(row, count), cols] = mixed.astype(BF16)
            return carry

        lax.fori_loop(0, HEADS, one_head, 0, unroll=True)

    chunk_rows = (512, 768, 256, 0)

    def half_rows(chunk, half):
        return pl.ds(chunk_rows[chunk] + half * HALF, HALF)

    def to_right(chunk, half):
        rows = half_rows(chunk, half)
        send(gbuf.at[0, rows], gbuf.at[3, rows], g_sent, g_r.at[chunk * 4 + (0, 2)[half]], along_y(1))

    def to_left(chunk, half):
        rows = half_rows(chunk, half)
        send(gbuf.at[0, rows], gbuf.at[1, rows], g_sent, g_r.at[chunk * 4 + (2, 1)[half]], along_y(3))

    def share(chunk):
        to_right(chunk, 0)
        to_left(chunk, 1)
        to_right(chunk, 1)
        to_left(chunk, 0)

    def relay(chunk):
        rows, at = half_rows(chunk, 0), chunk * 4
        wait_bytes(gbuf.at[3, rows], g_r.at[at])
        send(gbuf.at[3, rows], gbuf.at[2, rows], g_sent, g_r.at[at + 3], along_y(1))
        rows = half_rows(chunk, 1)
        wait_bytes(gbuf.at[1, rows], g_r.at[at + 1])
        send(gbuf.at[1, rows], gbuf.at[2, rows], g_sent, g_r.at[at + 3], along_y(3))

    def adjacent(chunk):
        wait_bytes(gbuf.at[1, pl.ds(chunk_rows[chunk], BLOCK)], g_r.at[chunk * 4 + 2])

    def opposite(chunk):
        wait_bytes(gbuf.at[2, pl.ds(chunk_rows[chunk], BLOCK)], g_r.at[chunk * 4 + 3])

    def product(rows, cols, owners):
        total = jnp.dot(gbuf[owners[0], rows], wbuf[owners[0], :, cols], preferred_element_type=F32)
        for j in owners[1:]:
            total += jnp.dot(gbuf[j, rows], wbuf[j, :, cols], preferred_element_type=F32)
        return total

    def tiles(one_tile):
        def step(n, carry):
            one_tile(pl.ds(pl.multiple_of(n * 256, 256), 256))
            return carry

        lax.fori_loop(0, COLS // 256, step, 0)

    def project(chunk):
        rows = pl.ds(chunk_rows[chunk], BLOCK)

        def one_tile(cols):
            out[rows, cols] = product(rows, cols, (0, 1, 2, 3)).astype(BF16)

        tiles(one_tile)

    def project_near(chunk, total):
        rows = pl.ds(chunk_rows[chunk], BLOCK)

        def one_tile(cols):
            total[:, cols] = product(rows, cols, (0, 1, 3))

        tiles(one_tile)

    def project_far(chunk, total):
        rows = pl.ds(chunk_rows[chunk], BLOCK)

        def one_tile(cols):
            out[rows, cols] = (total[:, cols] + product(rows, cols, (2,))).astype(BF16)

        tiles(one_tile)

    finish(512, HALF)
    to_right(0, 0)
    to_left(0, 0)
    finish(512 + HALF, HALF)
    to_right(0, 1)
    to_left(0, 1)
    finish(768, BLOCK)
    share(1)
    wait_bytes(weight_half(1, 0), w_r.at[1])
    pass_weights(1, 0, 3, along_x(1))
    wait_bytes(weight_half(3, 1), w_r.at[2])
    pass_weights(3, 1, 3, along_x(3))
    band_arrived(0)
    attend(0, 1)
    relay(0)
    finish(256, BLOCK)
    share(2)
    relay(1)
    band_arrived(1)
    attend(0, 0)
    finish(0, BLOCK)
    share(3)

    wait_bytes(wbuf.at[foreign, pl.ds(0, 128)], w_r.at[3])
    for d in range(1, GROUP):
        rows = piece_rows(d, core)
        send(wbuf.at[foreign, rows], wbuf.at[foreign, rows], wc_sent, w_r.at[4], partner)
    wait_bytes(wbuf.at[foreign, pl.ds(0, 256)], w_r.at[4])
    load_w.wait()

    adjacent(0)
    opposite(0)
    project(0)
    relay(2)
    adjacent(1)
    opposite(1)
    project(1)
    relay(3)
    adjacent(2)
    project_near(2, bias)
    adjacent(3)
    project_near(3, near_sum)
    opposite(2)
    project_far(2, bias)
    opposite(3)
    project_far(3, near_sum)
    wait_bytes(slices_in.at[pl.ds(0, ROW - 1)], state_sent)
    wait_bytes(mem_in.at[pl.ds(0, ROW - 1)], mem_sent)
    wait_bytes(wbuf.at[foreign, own_rows], wy_sent)
    wait_bytes(wbuf.at[foreign, pl.ds(0, 192)], wx_sent)
    wait_bytes(wbuf.at[foreign, pl.ds(0, 256)], wc_sent)
    wait_bytes(kbuf.at[pl.ds(0, 4 * BLOCK)], band_sent)
    wait_bytes(gbuf.at[foreign], g_sent)
    for d in range(1, GROUP):
        pl.when(x + d < GROUP)(total_copy(d).wait_send)


def body(queries, keys, values, span_bounds, mem_decay, mem_gate, out_weight):
    anywhere = pl.BlockSpec(memory_space=pl.ANY)
    dma = pltpu.SemaphoreType.DMA
    return pl.pallas_call(
        kernel,
        out_shape=pltpu.VMEM((SEG, COLS), BF16),
        in_specs=[anywhere] * 7,
        out_specs=pl.BlockSpec(memory_space=pltpu.VMEM),
        scratch_shapes=[
            pltpu.SMEM((2, 64), jnp.int32),
            pltpu.SMEM((HEADS, GROUP * ROW), F32),
            pltpu.SMEM((HEADS,), F32),
            pltpu.VMEM((BAND + SEG, HEADS * WIDTH), BF16),
            pltpu.VMEM((BAND + SEG, HEADS * WIDTH), BF16),
            pltpu.VMEM((SEG, HEADS * WIDTH), BF16),
            pltpu.VMEM((GROUP, SEG, HEADS * WIDTH), BF16),
            pltpu.VMEM((GROUP, HEADS * WIDTH, COLS), BF16),
            pltpu.VMEM((SEG, HEADS * WIDTH), F32),
            pltpu.VMEM((BLOCK, 2 * PART), F32),
            pltpu.VMEM((BLOCK, COLS), F32),
            pltpu.VMEM((HEADS, 2 * WIDTH, WIDTH), BF16),
            pltpu.VMEM((HEADS, WIDTH, 2 * WIDTH), F32),
            pltpu.VMEM((HEADS, 8, WIDTH), F32),
            pltpu.VMEM((ROW, SLICE, WIDTH), BF16),
            pltpu.VMEM((ROW, SLICE, WIDTH), BF16),
            pltpu.VMEM((SLICE, WIDTH), BF16),
            pltpu.VMEM((GROUP, SLICE, WIDTH), BF16),
            pltpu.VMEM((ROW, SLICE, WIDTH), BF16),
            pltpu.VMEM((ROW, SLICE, WIDTH), BF16),
            dma((10,)), dma((3,)), dma((7,)), dma((4,)), dma((4,)),
            dma((2,)), dma((5,)), dma((2,)), dma((16,)),
        ],
        compiler_params=pltpu.CompilerParams(
            collective_id=0, has_side_effects=True, vmem_limit_bytes=60 * 1024 * 1024
        ),
    )(span_bounds.T, mem_decay.T, mem_gate, queries, keys, values, out_weight)


def solution(mesh):
    return jax.shard_map(
        body,
        mesh=mesh,
        in_specs=(
            P("seq", "head"),
            P("seq", "head"),
            P("seq", "head"),
            P(),
            P(None, "head"),
            P("head"),
            P("head", None),
        ),
        out_specs=P("seq", "head"),
        check_vma=False,
    )
```

time: 64.3 us -> 58.3 us (0.907)
  the two profiles are of different devices: /device:TPU:0 before, /device:TPU:1 now
where the time goes in v3:
time: 58.3 us; the launch traced here: 58.1 us
  Pallas kernels  56.8 us (97%)
  local copies, waits for them, and re-layouts  1.32 us (2%)
    pallas_call x1, Pallas kernels, body(): pl.pallas_call(kernel, out_shape=pltpu.VMEM((SEG, COLS), BF16), in_specs=...  56.8 us
    unnamed x1, local copies, waits for them, and re-layouts  1.32 us

profile of v3, /device:TPU:1, one launch (start us, length us, event | category | flops | bytes accessed | tf_op | source)
XLA Modules:
  0.0 58.1 jit_solution(93968491237103626)
XLA Ops:
  0.0 56.8 %shard_map.73 = bf16[1024,1024]{1,0:T(8,128)(2,1)S(1)} custom-call(s32[2,64]{1,0:T(2,128)} %bitcast.3, f32[4,32]{1,0:T(4,128)} %bitcast.2, f32[4]{0:T(128)} %gate_hbm.1, bf16[1024,512]{1,0:T(8,128)(2,1)} %q_hbm.1, bf16[1024,512]{1,0:T(8,128)(2,1)} %k_hbm.1, bf16[1024,512]{1,0:T(8,128)(2,1)} %v_hbm.1, bf16[512,4096]{1,0:T(8,128)(2,1)} %w_hbm.1), custom_call_target="tpu_custom_call" | custom-call | tf_op jit(solution)/shard_map/pallas_call | solution.py:389
  56.8 1.3 %copy.9 = bf16[1024,1024]{1,0:T(8,128)(2,1)} copy(bf16[1024,1024]{1,0:T(8,128)(2,1)S(1)} %shard_map.73) | data formatting | bytes 4194304

commit v4 on v3

--- a/solution.py
+++ b/solution.py
@@ -49,14 +49,13 @@
 def kernel(
     spans_hbm, decay_hbm, gate_hbm, q_hbm, k_hbm, v_hbm, w_hbm, out,
     spans, decay, gate, kbuf, vbuf, qbuf, gbuf, wbuf, local, bias, near_sum, mem, state_sum, key_sum,
-    slices_out, slices_in, total_out, totals_in, mem_out, mem_in,
-    load_sem, small_sem, send_sem, b_s, b_r, recv_sem, w_r, band_r, g_r,
+    slices_out, slices_in, total_out, totals_in, mem_out, mem_in, edge,
+    load_sem, small_sem, send_sem, b_s, b_r, recv_sem, w_r, band_r, g_r, edge_r,
 ):
     seq = lax.axis_index("seq")
     head = lax.axis_index("head")
     x, place = seq // ROW, seq % ROW
     core, z = seq % 2, (seq % ROW) // 2
-    n_seq = GROUP * ROW
 
     def along_y(d):
         return (seq, (head + d) % GROUP)
@@ -68,8 +67,9 @@
         return (x * ROW + (place + d) % ROW, head)
 
     partner = (seq + 1 - 2 * core, head)
-    following, previous = ((seq + 1) % n_seq, head), ((seq + n_seq - 1) % n_seq, head)
-    state_sent, mem_sent, wy_sent, wx_sent, wc_sent, band_sent, g_sent = (send_sem.at[n] for n in range(7))
+    state_sent, mem_sent, wy_sent, wx_sent, wc_sent, band_sent, g_sent, edge_sent = (
+        send_sem.at[n] for n in range(8)
+    )
 
     def send(src, dst, send_sem, recv_sem, device):
         pltpu.make_async_remote_copy(
@@ -84,6 +84,8 @@
         pltpu.make_async_copy(src, dst, small_sem.at[n])
         for n, (src, dst) in enumerate(((spans_hbm, spans), (decay_hbm, decay), (gate_hbm, gate)))
     ]
+    for copy in small:
+        copy.start()
     loads = []
     for t in range(SEG // BLOCK):
         for hbm, ref in ((k_hbm, kbuf), (v_hbm, vbuf)):
@@ -100,7 +102,7 @@
 
     barrier = pltpu.get_barrier_semaphore()
     sources = [along_y(d) for d in range(1, GROUP)] + [along_x(d) for d in range(1, GROUP)]
-    sources += [along_row(d) for d in range(1, ROW)] + [previous]
+    sources += [along_row(d) for d in range(1, ROW)]
     for device in sources:
         pl.semaphore_signal(barrier, inc=1, device_id=device, device_id_type=MESH)
 
@@ -113,6 +115,23 @@
         hbm, ref = (k_hbm, kbuf) if n % 2 == 0 else (v_hbm, vbuf)
         rows = BLOCK - (n // 2) * BLOCK
         return hbm.at[pl.ds(SEG - BAND + rows, BLOCK)], ref.at[pl.ds(rows, BLOCK)]
+
+    def over_edge(pieces):
+        for n in pieces:
+            send(band_piece(n)[0], edge.at[n], edge_sent, edge_r.at[n], along_x(1))
+
+    def pass_band(half):
+        for n in (2 * half, 2 * half + 1):
+            src, dst = band_piece(n)
+
+            @pl.when(place == ROW - 1)
+            def _():
+                wait_bytes(edge.at[n], edge_r.at[n])
+                send(edge.at[n], dst, band_sent, band_r.at[half], along_row(1))
+
+            @pl.when(place < ROW - 1)
+            def _():
+                send(src, dst, band_sent, band_r.at[half], along_row(1))
 
     def band_arrived(half):
         wait_bytes(kbuf.at[pl.ds(0, 2 * BLOCK)], band_r.at[half])
@@ -122,16 +141,15 @@
     for t in range(SEG // BLOCK):
         loads[2 * t].wait()
         loads[2 * t + 1].wait()
+        if t == SEG // BLOCK - 1:
+            load_q.start()
         rows = pl.ds(BAND + t * BLOCK, BLOCK)
         for h in range(HEADS):
             cols = pl.ds(h * WIDTH, WIDTH)
             feats = feature_map(kbuf[rows, cols].astype(F32))
             state_sum[h] += dot_first(vbuf[rows, cols], jnp.concatenate(two_terms(feats), axis=1))
             key_sum[h] += jnp.sum(feats.reshape(BLOCK // 8, 8, WIDTH), axis=0)
-    load_q.start()
     load_w.start()
-    for copy in small:
-        copy.start()
     for h in range(HEADS):
         state = (state_sum[h, :, :WIDTH] + state_sum[h, :, WIDTH:]).astype(BF16)
         sums = jnp.sum(key_sum[h], axis=0, keepdims=True)
@@ -181,6 +199,7 @@
 
         lax.fori_loop(0, HEADS, one_head, 0)
 
+    pl.when(place == ROW - 1)(functools.partial(over_edge, (0,)))
     attend(1, 0)
 
     wait_bytes(slices_in.at[pl.ds(0, ROW - 1)], recv_sem.at[0])
@@ -198,25 +217,29 @@
     for d in range(1, GROUP):
         pl.when(x + d < GROUP)(total_copy(d).start)
 
+    def send_memory():
+        for d in range(1, GROUP):
+            pl.when(x >= d)(functools.partial(wait_bytes, total_out, b_r.at[d]))
+        memory = jnp.zeros((SLICE, WIDTH), F32)
+        for n in range(GROUP):
+            factor = decay[z, n * ROW]
+            for t in range(1, ROW):
+                factor = factor * decay[z, n * ROW + t]
+            memory = jnp.where(n < x, factor * memory + totals_in[n].astype(F32), memory)
+        for t in range(ROW):
+            mem_out[t] = memory.astype(BF16)
+            memory = decay[z, x * ROW + t] * memory + slices_in[t].astype(F32)
+        for d in range(1, ROW):
+            send(
+                mem_out.at[(place + d) % ROW], mem_in.at[place], mem_sent, recv_sem.at[1], along_row(d)
+            )
+        mem_in[place] = mem_out[place]
+
+    pl.when(x == 0)(send_memory)
     attend(1, 1)
-
-    for d in range(1, GROUP):
-        pl.when(x >= d)(functools.partial(wait_bytes, total_out, b_r.at[d]))
-    memory = jnp.zeros((SLICE, WIDTH), F32)
-    for n in range(GROUP):
-        product = decay[z, n * ROW]
-        for t in range(1, ROW):
-            product = product * decay[z, n * ROW + t]
-        memory = jnp.where(n < x, product * memory + totals_in[n].astype(F32), memory)
-    for t in range(ROW):
-        mem_out[t] = memory.astype(BF16)
-        memory = decay[z, x * ROW + t] * memory + slices_in[t].astype(F32)
-    for d in range(1, ROW):
-        send(mem_out.at[(place + d) % ROW], mem_in.at[place], mem_sent, recv_sem.at[1], along_row(d))
-    mem_in[place] = mem_out[place]
+    pl.when(x > 0)(send_memory)
+    pl.when(place == ROW - 1)(functools.partial(over_edge, (1, 2, 3)))
     foreign = pl.ds(1, GROUP - 1)
-    wait_bytes(wbuf.at[foreign, own_rows], w_r.at[0])
-
     def pass_weights(d, half, at, device):
         piece = weight_half(d, half)
         send(piece, piece, wx_sent, w_r.at[at], device)
@@ -225,15 +248,10 @@
         row = (((x + GROUP - d) % GROUP) * 2 + core) * 64 + 32 * half
         return wbuf.at[foreign, pl.ds(pl.multiple_of(row, 32), 32)]
 
-    for half in (0, 1):
-        pass_weights(0, half, (1, 3)[half], along_x(1))
-        pass_weights(0, 1 - half, (2, 3)[half], along_x(3))
-    send(wbuf.at[foreign, own_rows], wbuf.at[foreign, own_rows], wc_sent, w_r.at[4], partner)
 
     wait_bytes(mem_in.at[pl.ds(0, ROW - 1)], recv_sem.at[1])
 
-    for n in range(4):
-        send(*band_piece(n), band_sent, band_r.at[n // 2], following)
+    pass_band(0)
 
     def place_memory(h, carry):
         mem[h, :64] = mem_in[2 * h, :64]
@@ -295,12 +313,12 @@
             total += jnp.dot(gbuf[j, rows], wbuf[j, :, cols], preferred_element_type=F32)
         return total
 
-    def tiles(one_tile):
+    def tiles(one_tile, unroll=False):
         def step(n, carry):
             one_tile(pl.ds(pl.multiple_of(n * 256, 256), 256))
             return carry
 
-        lax.fori_loop(0, COLS // 256, step, 0)
+        lax.fori_loop(0, COLS // 256, step, 0, unroll=unroll)
 
     def project(chunk):
         rows = pl.ds(chunk_rows[chunk], BLOCK)
@@ -324,7 +342,7 @@
         def one_tile(cols):
             out[rows, cols] = (total[:, cols] + product(rows, cols, (2,))).astype(BF16)
 
-        tiles(one_tile)
+        tiles(one_tile, unroll=True)
 
     finish(512, HALF)
     to_right(0, 0)
@@ -332,17 +350,23 @@
     finish(512 + HALF, HALF)
     to_right(0, 1)
     to_left(0, 1)
+    wait_bytes(wbuf.at[foreign, own_rows], w_r.at[0])
+    for half in (0, 1):
+        pass_weights(0, half, (1, 3)[half], along_x(1))
+        pass_weights(0, 1 - half, (2, 3)[half], along_x(3))
+    send(wbuf.at[foreign, own_rows], wbuf.at[foreign, own_rows], wc_sent, w_r.at[4], partner)
     finish(768, BLOCK)
     share(1)
+    pass_band(1)
+    relay(0)
+    band_arrived(0)
+    attend(0, 1)
+    finish(256, BLOCK)
+    share(2)
     wait_bytes(weight_half(1, 0), w_r.at[1])
     pass_weights(1, 0, 3, along_x(1))
     wait_bytes(weight_half(3, 1), w_r.at[2])
     pass_weights(3, 1, 3, along_x(3))
-    band_arrived(0)
-    attend(0, 1)
-    relay(0)
-    finish(256, BLOCK)
-    share(2)
     relay(1)
     band_arrived(1)
     attend(0, 0)
@@ -381,6 +405,7 @@
     wait_bytes(gbuf.at[foreign], g_sent)
     for d in range(1, GROUP):
         pl.when(x + d < GROUP)(total_copy(d).wait_send)
+    pl.when(place == ROW - 1)(functools.partial(wait_bytes, edge, edge_sent))
 
 
 def body(queries, keys, values, span_bounds, mem_decay, mem_gate, out_weight):
@@ -412,8 +437,9 @@
             pltpu.VMEM((GROUP, SLICE, WIDTH), BF16),
             pltpu.VMEM((ROW, SLICE, WIDTH), BF16),
             pltpu.VMEM((ROW, SLICE, WIDTH), BF16),
-            dma((10,)), dma((3,)), dma((7,)), dma((4,)), dma((4,)),
-            dma((2,)), dma((5,)), dma((2,)), dma((16,)),
+            pltpu.VMEM((4, BLOCK, HEADS * WIDTH), BF16),
+            dma((10,)), dma((3,)), dma((8,)), dma((4,)), dma((4,)),
+            dma((2,)), dma((5,)), dma((2,)), dma((16,)), dma((4,)),
         ],
         compiler_params=pltpu.CompilerParams(
             collective_id=0, has_side_effects=True, vmem_limit_bytes=60 * 1024 * 1024

time: 58.3 us -> 55.9 us (0.959)
  the two profiles are of different devices: /device:TPU:1 before, /device:TPU:4 now
where the time goes in v4:
time: 55.9 us; the launch traced here: 55.8 us
  Pallas kernels  54.4 us (97%)
  local copies, waits for them, and re-layouts  1.32 us (2%)
    pallas_call x1, Pallas kernels, body(): pl.pallas_call(kernel, out_shape=pltpu.VMEM((SEG, COLS), BF16), in_specs=...  54.4 us
    unnamed x1, local copies, waits for them, and re-layouts  1.32 us

profile of v4, /device:TPU:4, one launch (start us, length us, event | category | flops | bytes accessed | tf_op | source)
XLA Modules:
  0.0 55.8 jit_solution(3768044312918411755)
XLA Ops:
  0.0 54.4 %shard_map.73 = bf16[1024,1024]{1,0:T(8,128)(2,1)S(1)} custom-call(s32[2,64]{1,0:T(2,128)} %bitcast.3, f32[4,32]{1,0:T(4,128)} %bitcast.2, f32[4]{0:T(128)} %gate_hbm.1, bf16[1024,512]{1,0:T(8,128)(2,1)} %q_hbm.1, bf16[1024,512]{1,0:T(8,128)(2,1)} %k_hbm.1, bf16[1024,512]{1,0:T(8,128)(2,1)} %v_hbm.1, bf16[512,4096]{1,0:T(8,128)(2,1)} %w_hbm.1), custom_call_target="tpu_custom_call" | custom-call | tf_op jit(solution)/shard_map/pallas_call | solution.py:414
  54.4 1.3 %copy.9 = bf16[1024,1024]{1,0:T(8,128)(2,1)} copy(bf16[1024,1024]{1,0:T(8,128)(2,1)S(1)} %shard_map.73) | data formatting | bytes 4194304

commit v5 on v4

--- a/solution.py
+++ b/solution.py
@@ -12,6 +12,7 @@
 BAND = 512
 PART = 512
 BLOCK = 256
+PIECE = 256
 HALF = 128
 HEADS = 4
 WIDTH = 128
@@ -86,18 +87,19 @@
     ]
     for copy in small:
         copy.start()
-    loads = []
-    for t in range(SEG // BLOCK):
+    for t in range(SEG // PIECE):
         for hbm, ref in ((k_hbm, kbuf), (v_hbm, vbuf)):
-            copy = pltpu.make_async_copy(
-                hbm.at[pl.ds(t * BLOCK, BLOCK)], ref.at[pl.ds(BAND + t * BLOCK, BLOCK)],
-                load_sem.at[len(loads)],
-            )
-            copy.start()
-            loads.append(copy)
-    load_q = pltpu.make_async_copy(q_hbm, qbuf, load_sem.at[8])
+            pltpu.make_async_copy(
+                hbm.at[pl.ds(t * PIECE, PIECE)], ref.at[pl.ds(BAND + t * PIECE, PIECE)], load_sem.at[t]
+            ).start()
+    first_rows, later_rows = pl.ds(PART, BLOCK), (pl.ds(0, PART), pl.ds(PART + BLOCK, BLOCK))
+    load_q = [
+        pltpu.make_async_copy(q_hbm.at[rows], qbuf.at[rows], load_sem.at[SEG // PIECE + n])
+        for n, rows in enumerate((first_rows, *later_rows))
+    ]
+    load_q[0].start()
     load_w = pltpu.make_async_copy(
-        w_hbm.at[:, pl.ds(pl.multiple_of(head * COLS, COLS), COLS)], wbuf.at[0], load_sem.at[9]
+        w_hbm.at[:, pl.ds(pl.multiple_of(head * COLS, COLS), COLS)], wbuf.at[0], load_sem.at[SEG // PIECE + 3]
     )
 
     barrier = pltpu.get_barrier_semaphore()
@@ -138,17 +140,14 @@
 
     state_sum[...] = jnp.zeros((HEADS, WIDTH, 2 * WIDTH), F32)
     key_sum[...] = jnp.zeros((HEADS, 8, WIDTH), F32)
-    for t in range(SEG // BLOCK):
-        loads[2 * t].wait()
-        loads[2 * t + 1].wait()
-        if t == SEG // BLOCK - 1:
-            load_q.start()
-        rows = pl.ds(BAND + t * BLOCK, BLOCK)
+    for t in range(SEG // PIECE):
+        wait_bytes(kbuf.at[pl.ds(0, 2 * PIECE)], load_sem.at[t])
+        rows = pl.ds(BAND + t * PIECE, PIECE)
         for h in range(HEADS):
             cols = pl.ds(h * WIDTH, WIDTH)
             feats = feature_map(kbuf[rows, cols].astype(F32))
             state_sum[h] += dot_first(vbuf[rows, cols], jnp.concatenate(two_terms(feats), axis=1))
-            key_sum[h] += jnp.sum(feats.reshape(BLOCK // 8, 8, WIDTH), axis=0)
+            key_sum[h] += jnp.sum(feats.reshape(PIECE // 8, 8, WIDTH), axis=0)
     load_w.start()
     for h in range(HEADS):
         state = (state_sum[h, :, :WIDTH] + state_sum[h, :, WIDTH:]).astype(BF16)
@@ -170,21 +169,24 @@
         )
     for copy in small:
         copy.wait()
-    load_q.wait()
-
-    def attend(part, sub):
+    load_q[0].wait()
+    load_q[1].start()
+    load_q[2].start()
+
+    def attend(part, sub, first_head=0, last_head=HEADS):
         row = part * PART + sub * BLOCK
         count = 2 * PART - sub * BLOCK
-        first = spans[0, 2 * seq + part] - seq * SEG
-        last = spans[1, 2 * seq + part] - seq * SEG
-        r = lax.broadcasted_iota(jnp.int32, (BLOCK, count), 0)
-        j = lax.broadcasted_iota(jnp.int32, (BLOCK, count), 1)
-        near = (j <= r + BAND) & (j > r)
-        key_at, query_at = j + (row - BAND), r + row
-        if part == 0:
-            near = near & (key_at >= jnp.where(seq > 0, -BAND, 0))
-        same = (query_at >= first) & (query_at < last) & (key_at >= first) & (key_at < last)
-        bias[:, :count] = jnp.where(near | same, 0.0, -1e30)
+        if first_head == 0:
+            first = spans[0, 2 * seq + part] - seq * SEG
+            last = spans[1, 2 * seq + part] - seq * SEG
+            r = lax.broadcasted_iota(jnp.int32, (BLOCK, count), 0)
+            j = lax.broadcasted_iota(jnp.int32, (BLOCK, count), 1)
+            near = (j <= r + BAND) & (j > r)
+            key_at, query_at = j + (row - BAND), r + row
+            if part == 0:
+                near = near & (key_at >= jnp.where(seq > 0, -BAND, 0))
+            same = (query_at >= first) & (query_at < last) & (key_at >= first) & (key_at < last)
+            bias[:, :count] = jnp.where(near | same, 0.0, -1e30)
 
         def one_head(h, carry):
             cols = head_columns(h)
@@ -197,7 +199,7 @@
             local[pl.ds(row, BLOCK), cols] = mixed / jnp.sum(weights, axis=1, keepdims=True)
             return carry
 
-        lax.fori_loop(0, HEADS, one_head, 0)
+        lax.fori_loop(first_head, last_head, one_head, 0)
 
     pl.when(place == ROW - 1)(functools.partial(over_edge, (0,)))
     attend(1, 0)
@@ -229,16 +231,19 @@
         for t in range(ROW):
             mem_out[t] = memory.astype(BF16)
             memory = decay[z, x * ROW + t] * memory + slices_in[t].astype(F32)
-        for d in range(1, ROW):
-            send(
-                mem_out.at[(place + d) % ROW], mem_in.at[place], mem_sent, recv_sem.at[1], along_row(d)
-            )
+        for n in range(ROW):
+            pl.when(place != n)(functools.partial(
+                send, mem_out.at[n], mem_in.at[place], mem_sent, recv_sem.at[1], (x * ROW + n, head)
+            ))
         mem_in[place] = mem_out[place]
 
     pl.when(x == 0)(send_memory)
-    attend(1, 1)
+    for copy in load_q[1:]:
+        copy.wait()
+    attend(1, 1, 0, 2)
     pl.when(x > 0)(send_memory)
     pl.when(place == ROW - 1)(functools.partial(over_edge, (1, 2, 3)))
+    attend(1, 1, 2, HEADS)
     foreign = pl.ds(1, GROUP - 1)
     def pass_weights(d, half, at, device):
         piece = weight_half(d, half)
@@ -250,8 +255,6 @@
 
 
     wait_bytes(mem_in.at[pl.ds(0, ROW - 1)], recv_sem.at[1])
-
-    pass_band(0)
 
     def place_memory(h, carry):
         mem[h, :64] = mem_in[2 * h, :64]
@@ -350,6 +353,7 @@
     finish(512 + HALF, HALF)
     to_right(0, 1)
     to_left(0, 1)
+    pass_band(0)
     wait_bytes(wbuf.at[foreign, own_rows], w_r.at[0])
     for half in (0, 1):
         pass_weights(0, half, (1, 3)[half], along_x(1))
@@ -438,7 +442,7 @@
             pltpu.VMEM((ROW, SLICE, WIDTH), BF16),
             pltpu.VMEM((ROW, SLICE, WIDTH), BF16),
             pltpu.VMEM((4, BLOCK, HEADS * WIDTH), BF16),
-            dma((10,)), dma((3,)), dma((8,)), dma((4,)), dma((4,)),
+            dma((8,)), dma((3,)), dma((8,)), dma((4,)), dma((4,)),
             dma((2,)), dma((5,)), dma((2,)), dma((16,)), dma((4,)),
         ],
         compiler_params=pltpu.CompilerParams(

time: 55.9 us -> 55.5 us (level)
  no operation moved by 1% of the time
where the time goes in v5:
time: 55.5 us; the launch traced here: 55.3 us
  Pallas kernels  54 us (97%)
  local copies, waits for them, and re-layouts  1.32 us (2%)
    pallas_call x1, Pallas kernels, body(): pl.pallas_call(kernel, out_shape=pltpu.VMEM((SEG, COLS), BF16), in_specs=...  54 us
    unnamed x1, local copies, waits for them, and re-layouts  1.32 us

profile of v5, /device:TPU:4, one launch (start us, length us, event | category | flops | bytes accessed | tf_op | source)
XLA Modules:
  0.0 55.3 jit_solution(8215092607621024810)
XLA Ops:
  0.0 54.0 %shard_map.73 = bf16[1024,1024]{1,0:T(8,128)(2,1)S(1)} custom-call(s32[2,64]{1,0:T(2,128)} %bitcast.3, f32[4,32]{1,0:T(4,128)} %bitcast.2, f32[4]{0:T(128)} %gate_hbm.1, bf16[1024,512]{1,0:T(8,128)(2,1)} %q_hbm.1, bf16[1024,512]{1,0:T(8,128)(2,1)} %k_hbm.1, bf16[1024,512]{1,0:T(8,128)(2,1)} %v_hbm.1, bf16[512,4096]{1,0:T(8,128)(2,1)} %w_hbm.1), custom_call_target="tpu_custom_call" | custom-call | tf_op jit(solution)/shard_map/pallas_call | solution.py:418
  54.0 1.3 %copy.9 = bf16[1024,1024]{1,0:T(8,128)(2,1)} copy(bf16[1024,1024]{1,0:T(8,128)(2,1)S(1)} %shard_map.73) | data formatting | bytes 4194304

commit v6 on v5

--- a/solution.py
+++ b/solution.py
@@ -48,8 +48,8 @@
 
 
 def kernel(
-    spans_hbm, decay_hbm, gate_hbm, q_hbm, k_hbm, v_hbm, w_hbm, out,
-    spans, decay, gate, kbuf, vbuf, qbuf, gbuf, wbuf, local, bias, near_sum, mem, state_sum, key_sum,
+    spans_hbm, decay_hbm, gate_hbm, q_hbm, k_hbm, v_hbm, w_hbm, out, near_sum, far_rows, far_weight,
+    spans, decay, gate, kbuf, vbuf, qbuf, gbuf, wbuf, local, bias, mem, state_sum, key_sum,
     slices_out, slices_in, total_out, totals_in, mem_out, mem_in, edge,
     load_sem, small_sem, send_sem, b_s, b_r, recv_sem, w_r, band_r, g_r, edge_r,
 ):
@@ -383,6 +383,8 @@
         send(wbuf.at[foreign, rows], wbuf.at[foreign, rows], wc_sent, w_r.at[4], partner)
     wait_bytes(wbuf.at[foreign, pl.ds(0, 256)], w_r.at[4])
     load_w.wait()
+    keep_w = pltpu.make_async_copy(wbuf.at[2], far_weight, load_sem.at[0])
+    keep_w.start()
 
     adjacent(0)
     opposite(0)
@@ -398,8 +400,9 @@
     project_near(3, near_sum)
     opposite(2)
     project_far(2, bias)
+    keep_w.wait()
     opposite(3)
-    project_far(3, near_sum)
+    far_rows[...] = gbuf[2, :BLOCK]
     wait_bytes(slices_in.at[pl.ds(0, ROW - 1)], state_sent)
     wait_bytes(mem_in.at[pl.ds(0, ROW - 1)], mem_sent)
     wait_bytes(wbuf.at[foreign, own_rows], wy_sent)
@@ -412,14 +415,32 @@
     pl.when(place == ROW - 1)(functools.partial(wait_bytes, edge, edge_sent))
 
 
+def write_out(mixed, near_sum, far_rows, far_weight, out, last, sems):
+    rest = pl.ds(BLOCK, SEG - BLOCK)
+    copy = pltpu.make_async_copy(mixed.at[rest], out.at[rest], sems.at[0])
+    copy.start()
+    for n in range(COLS // 256):
+        cols = pl.ds(n * 256, 256)
+        far = jnp.dot(far_rows[...], far_weight[:, cols], preferred_element_type=F32)
+        last[:, cols] = (near_sum[:, cols] + far).astype(BF16)
+    tail = pltpu.make_async_copy(last, out.at[pl.ds(0, BLOCK)], sems.at[1])
+    tail.start()
+    copy.wait()
+    tail.wait()
+
+
 def body(queries, keys, values, span_bounds, mem_decay, mem_gate, out_weight):
     anywhere = pl.BlockSpec(memory_space=pl.ANY)
     dma = pltpu.SemaphoreType.DMA
-    return pl.pallas_call(
+    operands = (span_bounds.T, mem_decay.T, mem_gate, queries, keys, values, out_weight)
+    parts = pl.pallas_call(
         kernel,
-        out_shape=pltpu.VMEM((SEG, COLS), BF16),
+        out_shape=(
+            pltpu.VMEM((SEG, COLS), BF16), pltpu.VMEM((BLOCK, COLS), F32),
+            pltpu.VMEM((BLOCK, HEADS * WIDTH), BF16), pltpu.VMEM((HEADS * WIDTH, COLS), BF16),
+        ),
         in_specs=[anywhere] * 7,
-        out_specs=pl.BlockSpec(memory_space=pltpu.VMEM),
+        out_specs=[pl.BlockSpec(memory_space=pltpu.VMEM)] * 4,
         scratch_shapes=[
             pltpu.SMEM((2, 64), jnp.int32),
             pltpu.SMEM((HEADS, GROUP * ROW), F32),
@@ -431,7 +452,6 @@
             pltpu.VMEM((GROUP, HEADS * WIDTH, COLS), BF16),
             pltpu.VMEM((SEG, HEADS * WIDTH), F32),
             pltpu.VMEM((BLOCK, 2 * PART), F32),
-            pltpu.VMEM((BLOCK, COLS), F32),
             pltpu.VMEM((HEADS, 2 * WIDTH, WIDTH), BF16),
             pltpu.VMEM((HEADS, WIDTH, 2 * WIDTH), F32),
             pltpu.VMEM((HEADS, 8, WIDTH), F32),
@@ -446,9 +466,17 @@
             dma((2,)), dma((5,)), dma((2,)), dma((16,)), dma((4,)),
         ],
         compiler_params=pltpu.CompilerParams(
-            collective_id=0, has_side_effects=True, vmem_limit_bytes=60 * 1024 * 1024
+            collective_id=0, has_side_effects=True, vmem_limit_bytes=52 * 1024 * 1024
         ),
-    )(span_bounds.T, mem_decay.T, mem_gate, queries, keys, values, out_weight)
+    )(*(pltpu.with_memory_space_constraint(a, pltpu.HBM) for a in operands))
+    return pl.pallas_call(
+        write_out,
+        out_shape=jax.ShapeDtypeStruct((SEG, COLS), BF16),
+        in_specs=[anywhere] + [pl.BlockSpec(memory_space=pltpu.VMEM)] * 3,
+        out_specs=anywhere,
+        scratch_shapes=[pltpu.VMEM((BLOCK, COLS), BF16), dma((2,))],
+        compiler_params=pltpu.CompilerParams(vmem_limit_bytes=8 * 1024 * 1024),
+    )(*parts)
 
 
 def solution(mesh):

time: 55.5 us -> 55.1 us (level)
  local copies, waits for them, and re-layouts: 1.32 us -> 0 us
  Pallas kernels: 54 us -> 54.9 us
    unnamed x1 -> x0, local copies, waits for them, and re-layouts: 1.32 us -> none
    pallas_call x1 -> x2, Pallas kernels: 54 us -> 54.9 us  [the longest x1 53.6 us: body(): pl.pallas_call(kernel, out_shape=(pltpu.VMEM((SEG, COLS), BF16), pltpu.VM...]
where the time goes in v6:
time: 55.1 us; the launch traced here: 54.9 us
  Pallas kernels  54.9 us (100%)
    pallas_call x1, Pallas kernels, body(): pl.pallas_call(kernel, out_shape=(pltpu.VMEM((SEG, COLS), BF16), pltpu.VM...  53.6 us
    pallas_call x1, Pallas kernels, body(): pl.pallas_call(write_out, out_shape=jax.ShapeDtypeStruct((SEG, COLS), BF1...  1.33 us

profile of v6, /device:TPU:4, one launch (start us, length us, event | category | flops | bytes accessed | tf_op | source)
XLA Modules:
  0.0 54.9 jit_solution(10216323486808024242)
XLA Ops:
  0.0 53.6 %shard_map.73 = (bf16[1024,1024]{1,0:T(8,128)(2,1)S(1)}, f32[256,1024]{1,0:T(8,128)S(1)}, bf16[256,512]{1,0:T(8,128)(2,1)S(1)}, bf16[512,1024]{1,0:T(8,128)(2,1)S(1)}) custom-call(s32[2,64]{1,0:T(2,128)} %bitcast.3, f32[4,32]{1,0:T(4,128)} %bitcast.2, f32[4]{0:T(128)} %gate_hbm.1, bf16[1024,512]{1,0:T(8,128)(2,1)} %q_hbm.1, bf16[1024,512]{1,0:T(8,128)(2,1)} %k_hbm.1, ...), custom_call_target="tpu_custom_call" | custom-call | tf_op jit(solution)/shard_map/pallas_call | solution.py:436
  53.6 1.3 %shard_map.74 = bf16[1024,1024]{1,0:T(8,128)(2,1)} custom-call(bf16[1024,1024]{1,0:T(8,128)(2,1)S(1)} %get-tuple-element.9.mixed, f32[256,1024]{1,0:T(8,128)S(1)} %get-tuple-element.10.near_sum, bf16[256,512]{1,0:T(8,128)(2,1)S(1)} %get-tuple-element.11.far_rows, bf16[512,1024]{1,0:T(8,128)(2,1)S(1)} %get-tuple-element.12.far_weight), custom_call_target="tpu_custom_call" | custom-call | tf_op jit(solution)/shard_map/pallas_call | solution.py:472

commit v7 on v6

--- a/solution.py
+++ b/solution.py
@@ -50,7 +50,7 @@
 def kernel(
     spans_hbm, decay_hbm, gate_hbm, q_hbm, k_hbm, v_hbm, w_hbm, out, near_sum, far_rows, far_weight,
     spans, decay, gate, kbuf, vbuf, qbuf, gbuf, wbuf, local, bias, mem, state_sum, key_sum,
-    slices_out, slices_in, total_out, totals_in, mem_out, mem_in, edge,
+    slices_out, slices_in, total_out, totals_in, mem_out, mem_in, edge, early,
     load_sem, small_sem, send_sem, b_s, b_r, recv_sem, w_r, band_r, g_r, edge_r,
 ):
     seq = lax.axis_index("seq")
@@ -254,6 +254,8 @@
         return wbuf.at[foreign, pl.ds(pl.multiple_of(row, 32), 32)]
 
 
+    for n, term in enumerate(two_terms(feature_map(qbuf[pl.ds(PART, HALF)].astype(F32)))):
+        early[n] = term
     wait_bytes(mem_in.at[pl.ds(0, ROW - 1)], recv_sem.at[1])
 
     def place_memory(h, carry):
@@ -264,10 +266,13 @@
 
     lax.fori_loop(0, HEADS, place_memory, 0)
 
-    def finish(row, count):
+    def finish(row, count, ready=False):
         def one_head(h, carry):
             cols = head_columns(h)
-            high, low = two_terms(feature_map(qbuf[pl.ds(row, count), cols].astype(F32)))
+            if ready:
+                high, low = early[0, :, cols], early[1, :, cols]
+            else:
+                high, low = two_terms(feature_map(qbuf[pl.ds(row, count), cols].astype(F32)))
             both = dot_last(high, mem[h]) + dot_last(low, mem[h])
             readout = both[:, :WIDTH] / (both[:, WIDTH:] + 1.0)
             mix = 1.0 / (1.0 + jnp.exp(-jnp.full((1, WIDTH), gate[h], F32)))
@@ -347,7 +352,7 @@
 
         tiles(one_tile, unroll=True)
 
-    finish(512, HALF)
+    finish(512, HALF, ready=True)
     to_right(0, 0)
     to_left(0, 0)
     finish(512 + HALF, HALF)
@@ -462,6 +467,7 @@
             pltpu.VMEM((ROW, SLICE, WIDTH), BF16),
             pltpu.VMEM((ROW, SLICE, WIDTH), BF16),
             pltpu.VMEM((4, BLOCK, HEADS * WIDTH), BF16),
+            pltpu.VMEM((2, HALF, HEADS * WIDTH), BF16),
             dma((8,)), dma((3,)), dma((8,)), dma((4,)), dma((4,)),
             dma((2,)), dma((5,)), dma((2,)), dma((16,)), dma((4,)),
         ],

time: 55.1 us -> 55 us (level)
  no operation moved by 1% of the time
where the time goes in v7:
time: 55 us; the launch traced here: 54.9 us
  Pallas kernels  54.9 us (100%)
    pallas_call x1, Pallas kernels, body(): pl.pallas_call(kernel, out_shape=(pltpu.VMEM((SEG, COLS), BF16), pltpu.VM...  53.6 us
    pallas_call x1, Pallas kernels, body(): pl.pallas_call(write_out, out_shape=jax.ShapeDtypeStruct((SEG, COLS), BF1...  1.33 us

profile of v7, /device:TPU:4, one launch (start us, length us, event | category | flops | bytes accessed | tf_op | source)
XLA Modules:
  0.0 54.9 jit_solution(4635576232783392322)
XLA Ops:
  0.0 53.6 %shard_map.73 = (bf16[1024,1024]{1,0:T(8,128)(2,1)S(1)}, f32[256,1024]{1,0:T(8,128)S(1)}, bf16[256,512]{1,0:T(8,128)(2,1)S(1)}, bf16[512,1024]{1,0:T(8,128)(2,1)S(1)}) custom-call(s32[2,64]{1,0:T(2,128)} %bitcast.3, f32[4,32]{1,0:T(4,128)} %bitcast.2, f32[4]{0:T(128)} %gate_hbm.1, bf16[1024,512]{1,0:T(8,128)(2,1)} %q_hbm.1, bf16[1024,512]{1,0:T(8,128)(2,1)} %k_hbm.1, ...), custom_call_target="tpu_custom_call" | custom-call | tf_op jit(solution)/shard_map/pallas_call | solution.py:441
  53.6 1.3 %shard_map.74 = bf16[1024,1024]{1,0:T(8,128)(2,1)} custom-call(bf16[1024,1024]{1,0:T(8,128)(2,1)S(1)} %get-tuple-element.9.mixed, f32[256,1024]{1,0:T(8,128)S(1)} %get-tuple-element.10.near_sum, bf16[256,512]{1,0:T(8,128)(2,1)S(1)} %get-tuple-element.11.far_rows, bf16[512,1024]{1,0:T(8,128)(2,1)S(1)} %get-tuple-element.12.far_weight), custom_call_target="tpu_custom_call" | custom-call | tf_op jit(solution)/shard_map/pallas_call | solution.py:478
